TPU v7x, 32 devices: a whole 2x2x4 slice. The times are simulated.
32 devices in a mesh: dp: 8 (over y, x, core), fsdp: 4 (over z).
Axes of the slice: x: 2, y: 2, z: 4, core: 2. Of those that a mesh axis runs over, the one named last changes fastest.
Arguments:
- tokens: bfloat16 [64, 1024, 768], P('dp', 'fsdp'), may hold values from -6 to 6
- cotangent: bfloat16 [64, 1024, 768], P('dp', 'fsdp'), may hold values from -6 to 6
- lengths: int32 [8, 8], P('dp'), may hold values from 256 to 1024, as said below
- perm: int32 [8, 8], P('dp'), may hold values from 0 to 7, each once within a row
- ln1_gain: bfloat16 [768], P(('dp', 'fsdp')), may hold values from 0.5 to 1.5
- ln1_bias: bfloat16 [768], P(('dp', 'fsdp')), may hold values from -3 to 3
- w_qkv: bfloat16 [768, 2304], P(('dp', 'fsdp')), may hold values from -0.3125 to 0.3125
- w_out: bfloat16 [768, 768], P(('dp', 'fsdp')), may hold values from -2.5 to 2.5
- ln2_gain: bfloat16 [768], P(('dp', 'fsdp')), may hold values from 0.5 to 1.5
- ln2_bias: bfloat16 [768], P(('dp', 'fsdp')), may hold values from -3 to 3
- w_up: bfloat16 [768, 3072], P(('dp', 'fsdp')), may hold values from -0.21875 to 0.21875
- w_down: bfloat16 [3072, 768], P(('dp', 'fsdp')), may hold values from -0.75 to 0.75
Outputs:
- block_out: bfloat16 [64, 1024, 768], P('dp', 'fsdp')
- d_tokens: bfloat16 [64, 1024, 768], P('dp', 'fsdp')
- grad_ln1_gain: float32 [768], P(('dp', 'fsdp'))
- grad_ln1_bias: float32 [768], P(('dp', 'fsdp'))
- grad_w_qkv: float32 [768, 2304], P(('dp', 'fsdp'))
- grad_w_out: float32 [768, 768], P(('dp', 'fsdp'))
- grad_ln2_gain: float32 [768], P(('dp', 'fsdp'))
- grad_ln2_bias: float32 [768], P(('dp', 'fsdp'))
- grad_w_up: float32 [768, 3072], P(('dp', 'fsdp'))
- grad_w_down: float32 [3072, 768], P(('dp', 'fsdp'))
Inputs may be any that keep to these rules, and one draw needn't show every extreme that they name: lengths[g, p] is the live length of sequence perm[g, p] of dp group g, dealt to fsdp index p // 2 as its micro-batch p % 2; each row holds 1024 and 256 at least once. `perm`: each row is a permutation of the group's 8 sequences.
All inputs are finite; a program needn't handle non-finite values.
Results may differ from a plain program's by a relative error of at most 0.014.
The roundings to bfloat16 on the way count: a program that leaves them out, or rounds other values in their place, can miss the bound.
Values may be sent and summed in bfloat16 or wider, within the bound.
No kernel may reach another device: no remote copies, remote signals or barrier semaphores. Data moves between devices by JAX's collectives and lax.ppermute only.
A program may use at most 384 MiB of HBM per device.

v0:
```python
import functools
import math

import jax
import jax.numpy as jnp
from jax import lax
from jax.experimental import pallas as pl
from jax.experimental.pallas import tpu as pltpu
from jax.sharding import PartitionSpec as P


DEPTH = 48
EPS = 1e-05
ROWS = 256
HALF = 128
GROUP = 3
BF = jnp.bfloat16
F32 = jnp.float32
ALPHA = 1.0 / math.sqrt(DEPTH)
GELU_C = 0.7978845608028654
GELU_A = 0.044715
VMEM_LIMIT = 60 * 1024 * 1024


def dot(a, b, ca=1, cb=0):
    return lax.dot_general(a, b, (((ca,), (cb,)), ((), ())), preferred_element_type=F32)


def norm(v):
    c = v - jnp.mean(v, axis=-1, keepdims=True)
    r = lax.rsqrt(jnp.mean(c * c, axis=-1, keepdims=True) + EPS)
    return c * r, r


def norm_back(f, n, r):
    return r * (f - jnp.mean(f, axis=-1, keepdims=True) - n * jnp.mean(f * n, axis=-1, keepdims=True))


def params(n):
    return pltpu.CompilerParams(
        dimension_semantics=("arbitrary",) * n, vmem_limit_bytes=VMEM_LIMIT
    )


def cost(micros, moved):
    return pl.CostEstimate(flops=int(micros * 1e9), transcendentals=0, bytes_accessed=moved)


def last_block(lens, m):
    return (lens[m] + (ROWS - 1)) // ROWS - 1


def attn_fwd_kernel(lens, x_ref, w_ref, vec_ref, qkv_ref, low_ref, lse_ref, kv_ref):
    m = pl.program_id(0)
    i = pl.program_id(1)
    d = x_ref.shape[2]
    live = i <= last_block(lens, m)

    @pl.when(live)
    def _():
        n, _ = norm(x_ref[0].astype(F32))
        low = (n * vec_ref[0:1, :] + vec_ref[1:2, :]).astype(BF)
        for t in range(3):
            part = dot(low, w_ref[:, t * d:(t + 1) * d]).astype(BF)
            qkv_ref[0, :, t * d:(t + 1) * d] = part
            if t:
                kv_ref[pl.ds(pl.multiple_of(i * ROWS, ROWS), ROWS), (t - 1) * d:t * d] = part

    part = lens[m] - i * ROWS <= HALF

    def variant(ii, size):
        keys = ii * ROWS + size

        @pl.when(live & (i == ii) & (part == (size == HALF)))
        def _():
            lane = lax.broadcasted_iota(jnp.int32, (size, 128), 1)
            row = lax.broadcasted_iota(jnp.int32, (size, size), 0)
            key = lax.broadcasted_iota(jnp.int32, (size, size), 1)
            allowed = (key <= row) & (key + ii * ROWS < lens[m])

            def group(gp, cols):
                spans, scores, values = [], [], []
                for sub in range(GROUP):
                    at = pl.multiple_of((gp * GROUP + sub) * 128, 128)
                    spans.append(pl.ds(at, 128))
                    q = qkv_ref[0, 0:size, pl.ds(at, 128)].astype(F32) * 0.125
                    k = kv_ref[0:keys, pl.ds(at, 128)]
                    values.append(kv_ref[0:keys, pl.ds(pl.multiple_of(d + at, 128), 128)])
                    for h in range(2):
                        qh = jnp.where((lane < 64) == (h == 0), q, 0.0).astype(BF)
                        scores.append(dot(qh, k, 1, 1))
                outs = []
                for n, s in enumerate(scores):
                    tail = jnp.where(allowed, s[:, ii * ROWS:], -1e30)
                    s = tail if ii == 0 else jnp.concatenate([s[:, :ii * ROWS], tail], axis=1)
                    peak = jnp.max(s, axis=-1, keepdims=True)
                    e = jnp.exp(s - peak)
                    total = jnp.sum(e, axis=-1, keepdims=True)
                    p = (e * (1.0 / total)).astype(BF)
                    outs.append(dot(p, values[n // 2]))
                    cols = jnp.where(lane == gp * (2 * GROUP) + n, peak + jnp.log(total), cols)
                for sub, span in enumerate(spans):
                    low_ref[0, 0:size, span] = jnp.where(lane < 64, outs[2 * sub], outs[2 * sub + 1]).astype(BF)
                return cols

            cols = lax.fori_loop(0, d // (128 * GROUP), group, jnp.zeros((size, 128), F32))
            lse_ref[0, :, 0:size] = jnp.transpose(cols)[0:16]

    for ii in range(x_rows_blocks(kv_ref)):
        variant(ii, ROWS)
        if ii:
            variant(ii, HALF)


def x_rows_blocks(ref):
    return ref.shape[0] // ROWS


def attn_fwd(lens, x, w, vec):
    mb, rows, d = x.shape
    nb = rows // ROWS

    def blk(m, i, ln):
        return (m, jnp.minimum(i, last_block(ln, m)), 0)

    return pl.pallas_call(
        attn_fwd_kernel,
        grid_spec=pltpu.PrefetchScalarGridSpec(
            num_scalar_prefetch=1,
            grid=(mb, nb),
            in_specs=[
                pl.BlockSpec((1, ROWS, d), blk),
                pl.BlockSpec((d, 3 * d), lambda m, i, ln: (0, 0), pipeline_mode=pl.Buffered(1)),
                pl.BlockSpec((8, d), lambda m, i, ln: (0, 0)),
            ],
            out_specs=[
                pl.BlockSpec((1, ROWS, 3 * d), blk),
                pl.BlockSpec((1, ROWS, d), blk),
                pl.BlockSpec((1, 16, ROWS), lambda m, i, ln: (m, 0, jnp.minimum(i, last_block(ln, m)))),
            ],
            scratch_shapes=[pltpu.VMEM((rows, 2 * d), BF)],
        ),
        out_shape=[
            jax.ShapeDtypeStruct((mb, rows, 3 * d), BF),
            jax.ShapeDtypeStruct((mb, rows, d), BF),
            jax.ShapeDtypeStruct((mb, 16, rows), F32),
        ],
        compiler_params=params(2),
        cost_estimate=cost(60, 20 << 20),
        name="attn_fwd",
    )(lens, x, w, vec)


def weight_copies(rest_ref, down_ref, wout_ref, wup_ref, wdown_ref, sem):
    d = wout_ref.shape[0]
    ff = wup_ref.shape[1]
    chunks = ff // d

    def out():
        return pltpu.make_async_copy(rest_ref.at[:, ff:ff + d], wout_ref, sem.at[2 * chunks])

    def up(c):
        at = pl.ds(pl.multiple_of(c * d, 128), d)
        return pltpu.make_async_copy(rest_ref.at[:, at], wup_ref.at[:, at], sem.at[c])

    def down(c):
        at = pl.ds(pl.multiple_of(c * d, 128), d)
        return pltpu.make_async_copy(down_ref.at[at, :], wdown_ref.at[at, :], sem.at[chunks + c])

    def start():
        out().start()
        for c in range(chunks):
            up(c).start()
            down(c).start()

    return start, out, up, down


def run_chunks(chunk, count, opening):
    if opening:
        lax.fori_loop(0, count, chunk, 0)
    else:
        for c in range(count):
            chunk(c, 0)


def mlp_fwd_kernel(lens, low_ref, x_ref, vec_ref, rest_ref, down_ref, out_ref, mid_ref,
                   wout_ref, wup_ref, wdown_ref, y_ref, sem):
    m = pl.program_id(0)
    i = pl.program_id(1)
    d = x_ref.shape[2]
    live = i <= last_block(lens, m)
    part = lens[m] - i * ROWS <= HALF
    first = (m == 0) & (i == 0)
    start, get_out, get_up, get_down = weight_copies(rest_ref, down_ref, wout_ref, wup_ref, wdown_ref, sem)

    @pl.when(first)
    def _():
        start()
        get_out().wait()

    @pl.when(jnp.logical_not(live))
    def _():
        out_ref[...] = jnp.zeros_like(out_ref)

    def body(size, opening):
        @pl.when(live & (part == (size == HALF)) & (first == opening))
        def _():
            alive = lax.broadcasted_iota(jnp.int32, (size, 1), 0) + i * ROWS < lens[m]
            middle = x_ref[0, 0:size].astype(F32) + ALPHA * dot(low_ref[0, 0:size], wout_ref[...])
            mid_ref[0, 0:size] = middle
            n2, _ = norm(middle)
            second = (n2 * vec_ref[2:3, :] + vec_ref[3:4, :]).astype(BF)
            y_ref[0:size] = jnp.zeros((size, d), F32)

            def chunk(c, carry):
                if opening:
                    get_up(c).wait()
                    get_down(c).wait()
                    at = pl.ds(pl.multiple_of(c * d, 128), d)
                else:
                    at = slice(c * d, (c + 1) * d)
                up = dot(second, wup_ref[:, at])
                t = jnp.tanh(GELU_C * (up + GELU_A * up * up * up))
                y_ref[0:size] += dot((up * (0.5 * (1.0 + t))).astype(BF), wdown_ref[at, :])
                return carry

            run_chunks(chunk, wup_ref.shape[1] // d, opening)
            out_ref[0, 0:size] = jnp.where(alive, middle + ALPHA * y_ref[0:size], 0.0).astype(BF)
            if size < ROWS:
                out_ref[0, size:] = jnp.zeros((ROWS - size, d), BF)

    body(ROWS, True)
    body(ROWS, False)
    body(HALF, False)


def mlp_fwd(lens, low, x, rest, wdown, vec):
    mb, rows, d = x.shape
    ff = wdown.shape[0]

    def blk(m, i, ln):
        return (m, jnp.minimum(i, last_block(ln, m)), 0)

    return pl.pallas_call(
        mlp_fwd_kernel,
        grid_spec=pltpu.PrefetchScalarGridSpec(
            num_scalar_prefetch=1,
            grid=(mb, rows // ROWS),
            in_specs=[
                pl.BlockSpec((1, ROWS, d), blk),
                pl.BlockSpec((1, ROWS, d), blk),
                pl.BlockSpec((8, d), lambda m, i, ln: (0, 0)),
                pl.BlockSpec(memory_space=pl.ANY),
                pl.BlockSpec(memory_space=pl.ANY),
            ],
            out_specs=[
                pl.BlockSpec((1, ROWS, d), lambda m, i, ln: (m, i, 0)),
                pl.BlockSpec((1, ROWS, d), blk),
            ],
            scratch_shapes=[
                pltpu.VMEM((d, d), BF),
                pltpu.VMEM((d, ff), BF),
                pltpu.VMEM((ff, d), BF),
                pltpu.VMEM((ROWS, d), F32),
                pltpu.SemaphoreType.DMA((2 * (ff // d) + 1,)),
            ],
        ),
        out_shape=[
            jax.ShapeDtypeStruct((mb, rows, d), BF),
            jax.ShapeDtypeStruct((mb, rows, d), F32),
        ],
        compiler_params=params(2),
        cost_estimate=cost(40, 40 << 20),
        name="mlp_fwd",
    )(lens, low, x, vec, rest, wdown)


def mlp_bwd_kernel(lens, low_ref, mid_ref, cot_ref, vec_ref, rest_ref, wd_ref,
                   gmid_ref, gmix_ref, inner_ref, gmain_ref, gdown_ref,
                   wout_ref, wup_ref, wdown_ref, aout_ref, aup_ref, adown_ref, gvec_ref, e2_ref,
                   stage_ref, down_ref, sem, *, share):
    m = pl.program_id(0)
    i = pl.program_id(1)
    d = mid_ref.shape[2]
    ff = wup_ref.shape[1]
    chunks = ff // d
    live = i <= last_block(lens, m)
    part = lens[m] - i * ROWS <= HALF
    first = (m == 0) & (i == 0)
    final = (m == pl.num_programs(0) - 1) & (i == pl.num_programs(1) - 1)
    start, get_out, get_up, get_down = weight_copies(rest_ref, wd_ref, wout_ref, wup_ref, wdown_ref, sem)

    @pl.when(first)
    def _():
        start()
        aout_ref[...] = jnp.zeros_like(aout_ref)
        aup_ref[...] = jnp.zeros_like(aup_ref)
        adown_ref[...] = jnp.zeros_like(adown_ref)
        gvec_ref[...] = jnp.zeros_like(gvec_ref)
        get_out().wait()

    def body(size):
        @pl.when(live & (part == (size == HALF)))
        def _():
            alive = lax.broadcasted_iota(jnp.int32, (size, 1), 0) + i * ROWS < lens[m]
            low = low_ref[0, 0:size]
            n2, r2 = norm(mid_ref[0, 0:size])
            gain = vec_ref[2:3, :]
            second = (n2 * gain + vec_ref[3:4, :]).astype(BF)
            second_t = jnp.transpose(second)
            gout = jnp.where(alive, cot_ref[0, 0:size].astype(F32), 0.0)
            gmlp = (ALPHA * gout).astype(BF)
            e2_ref[0:size] = jnp.zeros((size, d), F32)

            def chunk(c, carry):
                @pl.when(first)
                def _():
                    get_up(c).wait()
                    get_down(c).wait()

                at = pl.ds(pl.multiple_of(c * d, 128), d)
                up = dot(second, wup_ref[:, at])
                back = dot(gmlp, wdown_ref[at, :], 1, 1)
                sq = up * up
                t = jnp.tanh(GELU_C * (up + GELU_A * sq * up))
                half = 0.5 * (1.0 + t)
                act = (up * half).astype(BF)
                slope = half + 0.5 * up * (1.0 - t * t) * (GELU_C * (1.0 + 3.0 * GELU_A * sq))
                gup = (back * slope).astype(BF)
                adown_ref[at, :] += dot(act, gmlp, 0, 0)
                e2_ref[0:size] += dot(gup, wup_ref[:, at], 1, 1)
                aup_ref[:, at] += dot(second_t, gup)
                return carry

            lax.fori_loop(0, chunks, chunk, 0)
            e2 = e2_ref[0:size]
            gvec_ref[0:1, :] += jnp.sum(e2 * n2, axis=0, keepdims=True)
            gvec_ref[1:2, :] += jnp.sum(e2, axis=0, keepdims=True)
            gmid = gout + norm_back(e2 * gain, n2, r2)
            gmid_ref[0, 0:size] = gmid
            gao = (ALPHA * gmid).astype(BF)
            gmix = dot(gao, wout_ref[...], 1, 1).astype(BF)
            aout_ref[...] += dot(low, gao, 0, 0)
            gmix_ref[0, 0:size] = gmix
            prod = gmix.astype(F32) * low.astype(F32)
            head = lax.broadcasted_iota(jnp.int32, (16, d), 0)
            lane = lax.broadcasted_iota(jnp.int32, (16, d), 1)
            pick = jnp.where(lane // 64 == head, 1.0, 0.0).astype(F32)
            inner_ref[0, :, 0:size] = lax.dot_general(
                pick, prod, (((1,), (1,)), ((), ())),
                preferred_element_type=F32, precision=lax.Precision.HIGHEST,
            )

    body(ROWS)
    body(HALF)

    @pl.when(final)
    def _():
        main = d + ff
        stage_ref[:, 0:d] = aout_ref[...].astype(BF)
        stage_ref[:, d:main] = aup_ref[...].astype(BF)
        send = pltpu.make_async_copy(stage_ref, gmain_ref, sem.at[0])
        send.start()
        if share % 8 == 0:

            def regroup(e, carry):
                for c in range(chunks):
                    at = 2 * chunks * share * e + c * share
                    one = adown_ref[pl.ds(pl.multiple_of(at, 8), share), :]
                    two = adown_ref[pl.ds(pl.multiple_of(at + chunks * share, 8), share), :]
                    both = jnp.concatenate([one, two], axis=0).astype(BF)
                    down_ref[pl.ds(pl.multiple_of(2 * share * e, 16), 2 * share), c * d:(c + 1) * d] = both
                return carry

            lax.fori_loop(0, d // (2 * share), regroup, 0)
        else:
            for c in range(chunks):
                down_ref[:, c * d:(c + 1) * d] = adown_ref[c * d:(c + 1) * d, :].astype(BF)
        down_ref[:, ff:ff + 128] = jnp.transpose(gvec_ref[...]).astype(BF)
        last = pltpu.make_async_copy(down_ref, gdown_ref, sem.at[1])
        last.start()
        send.wait()
        last.wait()


def mlp_bwd(lens, low, mid, cot, rest, wdown, vec, share):
    mb, rows, d = mid.shape
    ff = wdown.shape[0]

    def blk(m, i, ln):
        return (m, jnp.minimum(i, last_block(ln, m)), 0)

    return pl.pallas_call(
        functools.partial(mlp_bwd_kernel, share=share),
        grid_spec=pltpu.PrefetchScalarGridSpec(
            num_scalar_prefetch=1,
            grid=(mb, rows // ROWS),
            in_specs=[
                pl.BlockSpec((1, ROWS, d), blk),
                pl.BlockSpec((1, ROWS, d), blk),
                pl.BlockSpec((1, ROWS, d), blk),
                pl.BlockSpec((8, d), lambda m, i, ln: (0, 0)),
                pl.BlockSpec(memory_space=pl.ANY),
                pl.BlockSpec(memory_space=pl.ANY),
            ],
            out_specs=[
                pl.BlockSpec((1, ROWS, d), blk),
                pl.BlockSpec((1, ROWS, d), blk),
                pl.BlockSpec((1, 16, ROWS), lambda m, i, ln: (m, 0, jnp.minimum(i, last_block(ln, m)))),
                pl.BlockSpec(memory_space=pl.ANY),
                pl.BlockSpec(memory_space=pl.ANY),
            ],
            scratch_shapes=[
                pltpu.VMEM((d, d), BF),
                pltpu.VMEM((d, ff), BF),
                pltpu.VMEM((ff, d), BF),
                pltpu.VMEM((d, d), F32),
                pltpu.VMEM((d, ff), F32),
                pltpu.VMEM((ff, d), F32),
                pltpu.VMEM((128, d), F32),
                pltpu.VMEM((ROWS, d), F32),
                pltpu.VMEM((d, d + ff), BF),
                pltpu.VMEM((d, ff + 128), BF),
                pltpu.SemaphoreType.DMA((2 * (ff // d) + 1,)),
            ],
        ),
        out_shape=[
            jax.ShapeDtypeStruct((mb, rows, d), F32),
            jax.ShapeDtypeStruct((mb, rows, d), BF),
            jax.ShapeDtypeStruct((mb, 16, rows), F32),
            jax.ShapeDtypeStruct((d, d + ff), BF),
            jax.ShapeDtypeStruct((d, ff + 128), BF),
        ],
        compiler_params=params(2),
        cost_estimate=cost(80, 60 << 20),
        name="mlp_bwd",
    )(lens, low, mid, cot, vec, rest, wdown)


def attn_bwd_kernel(lens, x_ref, q_ref, k_ref, v_ref, gmix_ref, gmid_ref, lse_ref, inner_ref,
                    w_ref, vec_ref, *rest, m, begin):
    if begin:
        dx_ref, gw_ref, acc_ref, gvec_ref, dk_ref, dv_ref, gq_ref = rest
    else:
        prev_ref, dx_ref, gw_ref, acc_ref, gvec_ref, dk_ref, dv_ref, gq_ref, before_ref, sem = rest
    g = pl.program_id(0)
    i = pl.num_programs(0) - 1 - g
    d = x_ref.shape[2]
    end = last_block(lens, m)
    live = i <= end

    @pl.when(g == 0)
    def _():
        if not begin:
            pltpu.make_async_copy(prev_ref, before_ref, sem).start()
        acc_ref[...] = jnp.zeros_like(acc_ref)
        gvec_ref[...] = jnp.zeros_like(gvec_ref)

    @pl.when(jnp.logical_not(live))
    def _():
        dx_ref[...] = jnp.zeros_like(dx_ref)

    part = lens[m] - i * ROWS <= HALF

    def variant(ii, size):
        keys = ii * ROWS + size

        @pl.when(live & (i == ii) & (part == (size == HALF)))
        def _():
            lane = lax.broadcasted_iota(jnp.int32, (size, 128), 1)
            key = lax.broadcasted_iota(jnp.int32, (size, size), 0)
            row = lax.broadcasted_iota(jnp.int32, (size, size), 1)
            allowed = (key <= row) & (key + ii * ROWS < lens[m])
            fresh = end == ii

            def group(gp, carry):
                spans, keep = [], []
                for sub in range(GROUP):
                    hp = gp * GROUP + sub
                    span = pl.ds(pl.multiple_of(hp * 128, 128), 128)
                    spans.append(span)
                    q = q_ref[0, 0:size, span].astype(F32) * 0.125
                    gm = gmix_ref[0, 0:size, span]
                    k = k_ref[0, 0:keys, span]
                    v = v_ref[0, 0:keys, span]
                    for h in range(2):
                        mine = (lane < 64) == (h == 0)
                        qh = jnp.where(mine, q, 0.0).astype(BF)
                        gh = jnp.where(mine, gm, jnp.zeros_like(gm))
                        keep.append((hp * 2 + h, qh, gh, dot(k, qh, 1, 1), dot(v, gh, 1, 1)))
                results = []
                for sub in range(GROUP):
                    k_t = jnp.transpose(k_ref[0, 0:keys, spans[sub]])
                    probs, grads, dqs = [], [], []
                    for h in range(2):
                        head, _, _, s, dp = keep[2 * sub + h]
                        tail = jnp.where(allowed, s[ii * ROWS:], -1e30)
                        s = tail if ii == 0 else jnp.concatenate([s[:ii * ROWS], tail], axis=0)
                        p = jnp.exp(s - lse_ref[0, pl.ds(head, 1), :][:, 0:size])
                        ds = (p * (dp - inner_ref[0, pl.ds(head, 1), :][:, 0:size])).astype(BF)
                        dqs.append(dot(k_t, ds)[h * 64:(h + 1) * 64])
                        probs.append(p.astype(BF))
                        grads.append(ds)
                    both = keep[2 * sub:2 * sub + 2]
                    dv = dot(jnp.concatenate(probs, axis=1), jnp.concatenate([b[2] for b in both], axis=0))
                    dk = dot(jnp.concatenate(grads, axis=1), jnp.concatenate([b[1] for b in both], axis=0))
                    dq = jnp.transpose(jnp.concatenate(dqs, axis=0)) * 0.125
                    results.append((dq, dk, dv))
                for span, (dq, dk, dv) in zip(spans, results):
                    gq_ref[0:size, span] = dq.astype(BF)
                    dv_ref[0:keys, span] = jnp.where(fresh, 0.0, dv_ref[0:keys, span]) + dv
                    dk_ref[0:keys, span] = jnp.where(fresh, 0.0, dk_ref[0:keys, span]) + dk
                return carry

            lax.fori_loop(0, d // (128 * GROUP), group, 0)

    for ii in range(x_rows_blocks(dk_ref)):
        variant(ii, ROWS)
        if ii:
            variant(ii, HALF)

    def finish(size):
        @pl.when(live & (part == (size == HALF)))
        def _():
            base = pl.ds(pl.multiple_of(i * ROWS, ROWS), size)
            gq_ref[0:size, d:2 * d] = dk_ref[base, :].astype(BF)
            gq_ref[0:size, 2 * d:] = dv_ref[base, :].astype(BF)
            n1, r1 = norm(x_ref[0, 0:size].astype(F32))
            gain = vec_ref[0:1, :]
            low_t = jnp.transpose((n1 * gain + vec_ref[1:2, :]).astype(BF))
            e1 = jnp.zeros((size, d), F32)
            for t in range(3):
                at = slice(t * d, (t + 1) * d)
                gq = gq_ref[0:size, at]
                e1 = e1 + dot(gq, w_ref[:, at], 1, 1)
                acc_ref[:, at] += dot(low_t, gq)
            gvec_ref[0:1, :] += jnp.sum(e1 * n1, axis=0, keepdims=True)
            gvec_ref[1:2, :] += jnp.sum(e1, axis=0, keepdims=True)
            alive = lax.broadcasted_iota(jnp.int32, (size, 1), 0) + i * ROWS < lens[m]
            dx = gmid_ref[0, 0:size] + norm_back(e1 * gain, n1, r1)
            dx_ref[0, 0:size] = jnp.where(alive, dx, 0.0).astype(BF)
            if size < ROWS:
                dx_ref[0, size:] = jnp.zeros((ROWS - size, d), BF)

    finish(ROWS)
    finish(HALF)

    @pl.when(i == 0)
    def _():
        total = acc_ref[...]
        rows = jnp.transpose(gvec_ref[...])
        if not begin:
            pltpu.make_async_copy(prev_ref, before_ref, sem).wait()
            total = total + before_ref[:, 0:3 * d].astype(F32)
            rows = rows + before_ref[:, 3 * d:].astype(F32)
        gw_ref[:, 0:3 * d] = total.astype(BF)
        gw_ref[:, 3 * d:] = rows.astype(BF)


def attn_bwd(m, prev, lens, x, qkv, gmix, gmid, lse, inner, gathered, vec):
    _, rows, d = x.shape
    nb = rows // ROWS
    begin = m == 0

    def blk(g, ln):
        return (m, jnp.minimum(nb - 1 - g, last_block(ln, m)), 0)

    def stat(g, ln):
        return (m, 0, jnp.minimum(nb - 1 - g, last_block(ln, m)))

    def fixed(g, ln):
        return (0, 0)

    one = pl.Buffered(1)
    whole = (d, 3 * d)
    wide = (d, 3 * d + 128)
    return pl.pallas_call(
        functools.partial(attn_bwd_kernel, m=m, begin=begin),
        grid_spec=pltpu.PrefetchScalarGridSpec(
            num_scalar_prefetch=1,
            grid=(nb,),
            in_specs=[
                pl.BlockSpec((1, ROWS, d), blk),
                pl.BlockSpec((1, ROWS, d), blk),
                pl.BlockSpec((1, rows, d), lambda g, ln: (m, 0, 1), pipeline_mode=one),
                pl.BlockSpec((1, rows, d), lambda g, ln: (m, 0, 2), pipeline_mode=one),
                pl.BlockSpec((1, ROWS, d), blk),
                pl.BlockSpec((1, ROWS, d), blk),
                pl.BlockSpec((1, 16, ROWS), stat),
                pl.BlockSpec((1, 16, ROWS), stat),
                pl.BlockSpec(whole, fixed, pipeline_mode=one),
                pl.BlockSpec((8, d), fixed),
            ] + ([] if begin else [pl.BlockSpec(memory_space=pl.ANY)]),
            out_specs=[
                pl.BlockSpec((1, ROWS, d), lambda g, ln: (0, nb - 1 - g, 0)),
                pl.BlockSpec(wide, fixed, pipeline_mode=one),
            ],
            scratch_shapes=[
                pltpu.VMEM(whole, F32),
                pltpu.VMEM((128, d), F32),
                pltpu.VMEM((rows, d), F32),
                pltpu.VMEM((rows, d), F32),
                pltpu.VMEM((ROWS, 3 * d), BF),
            ] + ([] if begin else [pltpu.VMEM(wide, BF), pltpu.SemaphoreType.DMA(())]),
        ),
        out_shape=[jax.ShapeDtypeStruct((1, rows, d), BF), jax.ShapeDtypeStruct(wide, BF)],
        compiler_params=params(1),
        cost_estimate=cost(40, 20 << 20),
        name="attn_bwd",
    )(lens, x, qkv, qkv, qkv, gmix, gmid, lse, inner, gathered, vec, *prev)


def place_blocks(table, pieces, blocks):
    each, rows, d = pieces[0].shape
    count = len(pieces)

    def kernel(at, *refs):
        srcs, out, held, sem = refs[:count], refs[count], refs[count + 1], refs[count + 2]
        slots = [(p, j, p * each + j) for p in range(count) for j in range(each)]
        loads = [pltpu.make_async_copy(srcs[p].at[j], held.at[k], sem.at[0, k]) for p, j, k in slots]
        stores = [pltpu.make_async_copy(held.at[k], out.at[at[k]], sem.at[1, k]) for p, j, k in slots]
        for c in loads:
            c.start()
        for load, store in zip(loads, stores):
            load.wait()
            store.start()
        for c in stores:
            c.wait()

    anywhere = pl.BlockSpec(memory_space=pl.ANY)
    return pl.pallas_call(
        kernel,
        grid_spec=pltpu.PrefetchScalarGridSpec(
            num_scalar_prefetch=1,
            grid=(1,),
            in_specs=[anywhere] * count,
            out_specs=anywhere,
            scratch_shapes=[
                pltpu.VMEM((count * each, rows, d), pieces[0].dtype),
                pltpu.SemaphoreType.DMA((2, count * each)),
            ],
        ),
        out_shape=jax.ShapeDtypeStruct((blocks, rows, d), pieces[0].dtype),
        compiler_params=params(1),
        cost_estimate=cost(4, 2 * blocks * rows * d * 2),
        name="place_blocks",
    )(table, *pieces)


def place_weights(table, sides, main, d):
    count, share, width = sides[0].shape
    chunks = (width - main) // d
    total = 2 * count * share

    def kernel(at, *refs):
        srcs, out, rest = refs[:2], refs[2], refs[3:]
        held, sem = rest[-2:]

        def load(side, k):
            return pltpu.make_async_copy(srcs[side].at[k], held.at[side, k], sem.at[side, k, chunks + 1])

        def stores(side, k):
            to = at[side * count + k]
            src = held.at[side, k]
            row = pl.ds(pl.multiple_of(to * share, 8), share)
            every = [pltpu.make_async_copy(src.at[:, 0:main], out.at[row, :], sem.at[side, k, 0])]
            for c in range(chunks):
                row = pl.ds(pl.multiple_of((to * chunks + c) * share, 8), share)
                col = slice(main + c * d, main + (c + 1) * d)
                every.append(pltpu.make_async_copy(src.at[:, col], rest[0].at[row, :], sem.at[side, k, c + 1]))
            return every

        for side in range(2):
            def begin(k, carry, side=side):
                load(side, k).start()
                return carry

            lax.fori_loop(0, count, begin, 0)
        for side in range(2):
            def turn(k, carry, side=side):
                load(side, k).wait()
                for c in stores(side, k):
                    c.start()
                return carry

            lax.fori_loop(0, count, turn, 0)
        for side in range(2):
            def end(k, carry, side=side):
                for c in stores(side, k):
                    c.wait()
                return carry

            lax.fori_loop(0, count, end, 0)

    anywhere = pl.BlockSpec(memory_space=pl.ANY)
    shapes = [jax.ShapeDtypeStruct((total, main), BF)]
    if chunks:
        shapes.append(jax.ShapeDtypeStruct((total * chunks, d), BF))
    return pl.pallas_call(
        kernel,
        grid_spec=pltpu.PrefetchScalarGridSpec(
            num_scalar_prefetch=1,
            grid=(1,),
            in_specs=[anywhere] * 2,
            out_specs=[anywhere] * len(shapes),
            scratch_shapes=[
                pltpu.VMEM((2, count, share, width), BF),
                pltpu.SemaphoreType.DMA((2, count, chunks + 2)),
            ],
        ),
        out_shape=shapes,
        compiler_params=params(1),
        cost_estimate=cost(8, 2 * total * width * 2),
        name="place_weights",
    )(table, *sides)


def swap(x, axis, bits):
    size = lax.axis_size(axis)
    return lax.ppermute(x, axis, [(s, s ^ bits) for s in range(size)])


def exchange(parts, axis):
    size = lax.axis_size(axis)
    return [parts[0]] + [swap(parts[b], axis, b) for b in range(1, size)]


def staged_gather(shard, main, d):
    dp = lax.axis_size("dp")
    zs = lax.axis_size("fsdp")
    chips = dp // 2
    got = jnp.stack(exchange([shard] * zs, "fsdp"))
    got = jnp.stack([got] + [swap(got, "dp", 2 * b) for b in range(1, chips)])
    share, width = shard.shape
    mine = got.reshape(chips * zs, share, width)
    other = swap(mine, "dp", 1)
    place = lax.axis_index("dp")
    z = lax.axis_index("fsdp")
    at = lax.iota(jnp.int32, chips * zs)
    table = jnp.concatenate([
        (place ^ (2 * (at // zs) + core)) * zs + (z ^ (at % zs)) for core in range(2)
    ])
    if share % 8 == 0:
        return place_weights(table, (mine, other), main, d)
    order = jnp.zeros_like(table).at[table].set(lax.iota(jnp.int32, dp * zs))
    whole = jnp.take(jnp.concatenate([mine, other]), order, axis=0, mode="clip")
    parts = [whole[:, :, :main].reshape(-1, main)]
    if width > main:
        down = whole[:, :, main:].reshape(dp * zs, share, -1, d).transpose(0, 2, 1, 3)
        parts.append(down.reshape(-1, d))
    return parts


def sum_partner(grads):
    dp = lax.axis_size("dp")
    block = grads.reshape(dp // 2, 2, -1, grads.shape[1])
    core = lax.axis_index("dp") % 2
    mine = lax.dynamic_index_in_dim(block, core, 1, keepdims=False)
    other = lax.dynamic_index_in_dim(block, 1 - core, 1, keepdims=False)
    return mine, swap(other, "dp", 1)


def sum_plane(mine, other):
    chip = lax.axis_index("dp") // 2

    def part(b):
        pick = [lax.dynamic_index_in_dim(t, chip ^ b, 0, keepdims=False) for t in (mine, other)]
        return (pick[0].astype(F32) + pick[1].astype(F32)).astype(BF)

    count = mine.shape[0]
    return [part(0)] + [swap(part(b), "dp", 2 * b) for b in range(1, count)]


def total_of(parts):
    acc = parts[0].astype(F32)
    for p in parts[1:]:
        acc = acc + p.astype(F32)
    return acc


def sum_line(parts):
    zs = lax.axis_size("fsdp")
    z = lax.axis_index("fsdp")
    low = total_of(parts).astype(BF)
    low = low.reshape(zs, -1, low.shape[1])
    pieces = [lax.dynamic_index_in_dim(low, z ^ b, 0, keepdims=False) for b in range(zs)]
    return total_of(exchange(pieces, "fsdp"))


def device_step(tokens, cotangent, lengths, perm, ln1_gain, ln1_bias, w_qkv, w_out,
               ln2_gain, ln2_bias, w_up, w_down):
    zs = lax.axis_size("fsdp")
    devices = lax.axis_size("dp") * zs
    z = lax.axis_index("fsdp")
    slots, rows, d = tokens.shape
    mb = slots // zs
    ff = w_up.shape[1]
    share = w_qkv.shape[0]
    chunks = ff // d
    dealing = perm[0]
    lens = lax.dynamic_slice_in_dim(lengths[0], z * mb, mb)
    order = (z ^ lax.iota(jnp.int32, zs))
    take_at = (order[:, None] * mb + lax.iota(jnp.int32, mb)[None, :]).reshape(-1)
    send_at = jnp.take(dealing, take_at, mode="clip")

    vectors = jnp.stack([ln1_gain, ln1_bias, ln2_gain, ln2_bias], axis=1)
    vectors = jnp.pad(vectors, ((0, 0), (0, 124)))
    down = w_down.reshape(chunks, share, d).transpose(1, 0, 2).reshape(share, ff)
    shard = jnp.concatenate([w_up, w_out, down], axis=1)
    (gathered,) = staged_gather(jnp.concatenate([w_qkv, vectors], axis=1), 3 * d + 128, d)
    rest, wdown = staged_gather(shard, ff + d, d)
    at = 3 * d
    vec = jnp.pad(jnp.transpose(gathered[:, at:at + 4]).astype(F32), ((0, 4), (0, 0)))

    def deal(array):
        parts = [jnp.take(array, send_at[b * mb:(b + 1) * mb], axis=0, mode="clip") for b in range(zs)]
        table = (lax.iota(jnp.int32, mb)[None, :] * zs + order[:, None]).reshape(-1)
        return place_blocks(table, exchange(parts, "fsdp"), slots).reshape(mb, zs * rows, d)

    def give_back(array):
        split = array.reshape(array.shape[0], zs, rows, d)
        parts = [lax.dynamic_index_in_dim(split, z ^ b, 1, keepdims=False) for b in range(zs)]
        return exchange(parts, "fsdp")

    x = deal(tokens)
    x, cotangent = lax.optimization_barrier((x, cotangent))
    cot = deal(cotangent)
    qkv, low, lse = attn_fwd(lens, x, gathered, vec)
    out, mid = mlp_fwd(lens, low, x, rest, wdown, vec)
    cot, out = lax.optimization_barrier((cot, out))
    gmid, gmix, inner, gmain, gdown = mlp_bwd(lens, low, mid, cot, rest, wdown, vec, share)
    if share % 8:
        gtop = gdown[:, :ff].reshape(d, chunks, d).transpose(1, 0, 2)
        gtop = gtop.reshape(devices, chunks, share, d).transpose(0, 2, 1, 3).reshape(d, ff)
        gdown = jnp.concatenate([gtop, gdown[:, ff:]], axis=1)
    early = lax.psum_scatter(gdown, ("dp", "fsdp"), scatter_dimension=0, tiled=True)
    halves = sum_partner(gmain)
    outs = give_back(out)
    grads = []
    prev = ()
    for m in range(mb):
        dx, gw = attn_bwd(m, prev, lens, x, qkv, gmix, gmid, lse, inner, gathered, vec)
        prev = (gw,)
        grads += give_back(dx)
        if m == 0:
            planes = sum_plane(*halves)
    halves = sum_partner(gw)
    late = sum_plane(*halves)
    late = sum_line(late)
    main = sum_line(planes)
    block_out = place_blocks(send_at, outs, slots)
    d_tokens = place_blocks(send_at.reshape(zs, mb).T.reshape(-1), grads, slots)
    early = early.astype(F32)
    g_down = early[:, :ff].reshape(share, chunks, d).transpose(1, 0, 2).reshape(share * chunks, d)
    return (
        block_out,
        d_tokens,
        late[:, 3 * d],
        late[:, 3 * d + 1],
        late[:, :3 * d],
        main[:, :d],
        early[:, ff],
        early[:, ff + 1],
        main[:, d:],
        g_down,
    )


def solution(mesh):
    wide = P(("dp", "fsdp"), None)
    thin = P(("dp", "fsdp"))
    seq = P("dp", "fsdp", None)
    group = P("dp", None)
    return jax.shard_map(
        device_step,
        mesh=mesh,
        in_specs=(seq, seq, group, group, thin, thin, wide, wide, thin, thin, wide, wide),
        out_specs=(seq, seq, thin, thin, wide, wide, thin, thin, wide, wide),
        check_vma=False,
    )
```

profile of v0, /device:TPU:0, one launch (start us, length us, event | category | flops | bytes accessed | tf_op | source)
XLA Modules:
  0.0 704.8 jit_solution(11627883034743646804)
XLA Ops:
  9.8 4.1 collective-permute-start.7
  20.0 2.8 collective-permute-start.1
  31.7 43.3 %collective-permute-done.6 = bf16[24,2432]{1,0:T(8,128)(2,1)S(1)} collective-permute-done((bf16[24,2432]{1,0:T(8,128)(2,1)}, bf16[24,2432]{1,0:T(8,128)(2,1)S(1)}, u32[]{:S(2)}, u32[]{:S(2)}) %collective-permute-start.6) | collective-permute-done | bytes 116768 | tf_op jit(solution)/shard_map/ppermute | solution.py:721
  76.9 2.1 fusion.18
  82.9 3.4 place_blocks.4
  89.8 24.8 %collective-permute-done.14 = bf16[24,6912]{1,0:T(8,128)(2,1)} collective-permute-done((bf16[24,6912]{1,0:T(8,128)(2,1)S(1)}, bf16[24,6912]{1,0:T(8,128)(2,1)}, u32[]{:S(2)}, u32[]{:S(2)}) %collective-permute-start.14) | collective-permute-done | bytes 331808 | tf_op jit(solution)/shard_map/ppermute | solution.py:721
  114.6 3.1 collective-permute-start.3
  117.7 5.8 collective-permute-start.4
  125.0 3.4 gather_fusion.8
  131.8 15.1 %collective-permute-done.3.refs_1_ = bf16[2,256,768]{2,1,0:T(8,128)(2,1)} collective-permute-done((bf16[2,256,768]{2,1,0:T(8,128)(2,1)}, bf16[2,256,768]{2,1,0:T(8,128)(2,1)}, u32[]{:S(2)}, u32[]{:S(2)}) %collective-permute-start.3) | collective-permute-done | bytes 786464 | tf_op jit(solution)/shard_map/ppermute | solution.py:721
  146.9 3.5 collective-permute-start.5
  150.4 2.8 pad_maximum_fusion.1
  153.3 22.7 %collective-permute-done.4.refs_2_ = bf16[2,256,768]{2,1,0:T(8,128)(2,1)} collective-permute-done((bf16[2,256,768]{2,1,0:T(8,128)(2,1)}, bf16[2,256,768]{2,1,0:T(8,128)(2,1)}, u32[]{:S(2)}, u32[]{:S(2)}) %collective-permute-start.4) | collective-permute-done | bytes 786464 | tf_op jit(solution)/shard_map/ppermute | solution.py:721
  177.1 3.4 gather_fusion.5
  180.5 3.5 place_blocks.5
  184.1 4.8 collective-permute-done.17
  188.9 5.3 pad_maximum_fusion
  194.2 4.8 place_weights.2.w_ref
  200.6 29.4 %attn_fwd.1 = (bf16[2,1024,2304]{2,1,0:T(8,128)(2,1)}, bf16[2,1024,768]{2,1,0:T(8,128)(2,1)}, f32[2,16,1024]{2,1,0:T(8,128)}) custom-call(s32[2]{0:T(128)} %fusion.16.lens, bf16[2,1024,768]{2,1,0:T(8,128)(2,1)} %bitcast.174, bf16[768,2432]{1,0:T(8,128)(2,1)} %place_weights.2.w_ref, f32[8,768]{1,0:T(8,128)} %pad_convert_fusion.vec_ref), custom_call_target="tpu_custom_call" | custom-call | flops 60000002048 | bytes 20971520 | tf_op jit(solution)/shard_map/attn_fwd/pallas_call | solution.py:126
  230.1 10.3 %place_weights.3 = (bf16[768,3840]{1,0:T(8,128)(2,1)}, bf16[3072,768]{1,0:T(8,128)(2,1)}) custom-call(s32[32]{0:T(128)} %pad_add_fusion.at, bf16[16,24,6912]{2,1,0:T(8,128)(2,1)} %bitcast.28.refs_0_, bf16[16,24,6912]{2,1,0:T(8,128)(2,1)} %collective-permute-done.19.refs_1_), custom_call_target="tpu_custom_call" | custom-call | flops 8000000000 | bytes 21233664 | tf_op jit(solution)/shard_map/place_weights/pallas_call | solution.py:700
  240.4 24.8 %mlp_fwd.1 = (bf16[2,1024,768]{2,1,0:T(8,128)(2,1)}, f32[2,1024,768]{2,1,0:T(8,128)}) custom-call(s32[2]{0:T(128)} %fusion.16.lens, bf16[2,1024,768]{2,1,0:T(8,128)(2,1)} %get-tuple-element.32.low_ref, bf16[2,1024,768]{2,1,0:T(8,128)(2,1)} %bitcast.175, f32[8,768]{1,0:T(8,128)} %pad_convert_fusion.vec_ref, bf16[768,3840]{1,0:T(8,128)(2,1)} %get-tuple-element.33.rest_ref, ...), custom_call_target="tpu_custom_call" | custom-call | flops 40000000000 | bytes 41943040 | tf_op jit(solution)/shard_map/mlp_fwd/pallas_call | solution.py:245
  265.1 60.0 %mlp_bwd.1 = (f32[2,1024,768]{2,1,0:T(8,128)}, bf16[2,1024,768]{2,1,0:T(8,128)(2,1)}, f32[2,16,1024]{2,1,0:T(8,128)}, bf16[768,3840]{1,0:T(8,128)(2,1)}, bf16[768,3200]{1,0:T(8,128)(2,1)}) custom-call(s32[2]{0:T(128)} %fusion.16.lens, bf16[2,1024,768]{2,1,0:T(8,128)(2,1)} %get-tuple-element.32.low_ref, f32[2,1024,768]{2,1,0:T(8,128)} %get-tuple-element.38.mid_ref, ...), custom_call_target="tpu_custom_call" | custom-call | flops 80000000000 | bytes 62914560 | tf_op jit(solution)/shard_map/mlp_bwd/pallas_call | solution.py:394
  325.2 3.6 dynamic-slice_bitcast_fusion
  329.3 38.3 %attn_bwd.2 = (bf16[1,1024,768]{2,1,0:T(8,128)(2,1)}, bf16[768,2432]{1,0:T(8,128)(2,1)}) custom-call(s32[2]{0:T(128)} %fusion.16.lens, bf16[2,1024,768]{2,1,0:T(8,128)(2,1)} %bitcast.176, bf16[2,1024,2304]{2,1,0:T(8,128)(2,1)} %get-tuple-element.37.q_ref.k_ref.v_ref, bf16[2,1024,2304]{2,1,0:T(8,128)(2,1)} %get-tuple-element.37.q_ref.k_ref.v_ref, ...), custom_call_target="tpu_custom_call" | custom-call | flops 40000000000 | bytes 20971520 | tf_op jit(solution)/shard_map/attn_bwd/pallas_call | solution.py:578
  367.6 28.2 %attn_bwd.3 = (bf16[1,1024,768]{2,1,0:T(8,128)(2,1)}, bf16[768,2432]{1,0:T(8,128)(2,1)}) custom-call(s32[2]{0:T(128)} %fusion.16.lens, bf16[2,1024,768]{2,1,0:T(8,128)(2,1)} %bitcast.177, bf16[2,1024,2304]{2,1,0:T(8,128)(2,1)} %get-tuple-element.37.q_ref.k_ref.v_ref, bf16[2,1024,2304]{2,1,0:T(8,128)(2,1)} %get-tuple-element.37.q_ref.k_ref.v_ref, ...), custom_call_target="tpu_custom_call" | custom-call | flops 40000000000 | bytes 20971520 | tf_op jit(solution)/shard_map/attn_bwd/pallas_call | solution.py:578
  395.8 2.2 dynamic-slice_bitcast_fusion.6
  398.0 49.9 %collective-permute-start.26 = (bf16[1,256,768]{2,1,0:T(8,128)(2,1)S(1)}, bf16[1,256,768]{2,1,0:T(8,128)(2,1)S(1)}, u32[]{:S(2)}, u32[]{:S(2)}) collective-permute-start(bf16[1,256,768]{2,1,0:T(8,128)(2,1)S(1)} %get-tuple-element.66), channel_id=1, source_target_pairs={{0,1},{1,0},{2,3},{3,2},{4,5},{5,4},{6,7},{7,6},{8,9},{9,8},{10,11... | collective-permute-start | bytes 1179656 | tf_op jit(solution)/shard_map/ppermute | solution.py:721
  447.9 22.3 %collective-permute-start.27 = (bf16[1,256,768]{2,1,0:T(8,128)(2,1)S(1)}, bf16[1,256,768]{2,1,0:T(8,128)(2,1)S(1)}, u32[]{:S(2)}, u32[]{:S(2)}) collective-permute-start(bf16[1,256,768]{2,1,0:T(8,128)(2,1)S(1)} %get-tuple-element.65), channel_id=1, source_target_pairs={{0,2},{1,3},{2,0},{3,1},{4,6},{5,7},{6,4},{7,5},{8,10},{9,11},{10,... | collective-permute-start | bytes 1179656 | tf_op jit(solution)/shard_map/ppermute | solution.py:721
  470.2 3.0 dynamic-slice_bitcast_fusion.1
  474.9 6.7 collective-permute-done.27.refs_6_
  481.6 6.5 collective-permute-done.28.refs_7_
  494.4 22.6 %collective-permute-start.20 = (bf16[2,256,768]{2,1,0:T(8,128)(2,1)}, bf16[2,256,768]{2,1,0:T(8,128)(2,1)S(1)}, u32[]{:S(2)}, u32[]{:S(2)}) collective-permute-start(bf16[2,256,768]{2,1,0:T(8,128)(2,1)} %get-tuple-element.62), channel_id=1, source_target_pairs={{0,1},{1,0},{2,3},{3,2},{4,5},{5,4},{6,7},{7,6},{8,9},{9,8},{10,11... | collective-permute-start | bytes 2359304 | tf_op jit(solution)/shard_map/ppermute | solution.py:721
  517.0 5.3 collective-permute-done.24.refs_2_
  522.3 9.1 %collective-permute-start.22 = (bf16[2,256,768]{2,1,0:T(8,128)(2,1)}, bf16[2,256,768]{2,1,0:T(8,128)(2,1)S(1)}, u32[]{:S(2)}, u32[]{:S(2)}) collective-permute-start(bf16[2,256,768]{2,1,0:T(8,128)(2,1)} %get-tuple-element.60), channel_id=1, source_target_pairs={{0,3},{1,2},{2,1},{3,0},{4,7},{5,6},{6,5},{7,4},{8,11},{9,10},{10,... | collective-permute-start | bytes 2359304 | tf_op jit(solution)/shard_map/ppermute | solution.py:721
  532.2 3.7 place_blocks.7
  535.9 54.9 %collective-permute-done.21.refs_2_ = bf16[2,256,768]{2,1,0:T(8,128)(2,1)S(1)} collective-permute-done((bf16[2,256,768]{2,1,0:T(8,128)(2,1)}, bf16[2,256,768]{2,1,0:T(8,128)(2,1)S(1)}, u32[]{:S(2)}, u32[]{:S(2)}) %collective-permute-start.21) | collective-permute-done | bytes 786464 | tf_op jit(solution)/shard_map/ppermute | solution.py:721
  591.9 3.4 place_blocks.6
  595.4 2.1 fusion.6
  597.5 6.0 collective-permute-start.30
  605.0 2.7 fusion.2
  607.8 2.0 collective-permute-start.37
  609.8 5.2 collective-permute-done.30
  615.0 12.8 %collective-permute-done.31 = bf16[96,2432]{1,0:T(8,128)(2,1)S(1)} collective-permute-done((bf16[96,2432]{1,0:T(8,128)(2,1)S(1)}, bf16[96,2432]{1,0:T(8,128)(2,1)S(1)}, u32[]{:S(2)}, u32[]{:S(2)}) %collective-permute-start.31) | collective-permute-done | bytes 466976 | tf_op jit(solution)/shard_map/ppermute | solution.py:721
  629.4 18.0 %collective-permute-start.33 = (bf16[24,2432]{1,0:T(8,128)(2,1)S(1)}, bf16[24,2432]{1,0:T(8,128)(2,1)S(1)}, u32[]{:S(2)}, u32[]{:S(2)}) collective-permute-start(bf16[24,2432]{1,0:T(8,128)(2,1)S(1)} %get-tuple-element.77), channel_id=1, source_target_pairs={{0,1},{1,0},{2,3},{3,2},{4,5},{5,4},{6,7},{7,6},{8,9},{9,8},{10,11... | collective-permute-start | bytes 350216 | tf_op jit(solution)/shard_map/ppermute | solution.py:721
  647.4 5.0 collective-permute-start.34
  655.7 19.5 %collective-permute-start.40 = (bf16[24,3840]{1,0:T(8,128)(2,1)S(1)}, bf16[24,3840]{1,0:T(8,128)(2,1)S(1)}, u32[]{:S(2)}, u32[]{:S(2)}) collective-permute-start(bf16[24,3840]{1,0:T(8,128)(2,1)S(1)} %get-tuple-element.74), channel_id=1, source_target_pairs={{0,1},{1,0},{2,3},{3,2},{4,5},{5,4},{6,7},{7,6},{8,9},{9,8},{10,11... | collective-permute-start | bytes 552968 | tf_op jit(solution)/shard_map/ppermute | solution.py:721
  675.2 2.4 collective-permute-start.42
  680.4 9.8 %collective-permute-done.41 = bf16[24,3840]{1,0:T(8,128)(2,1)S(1)} collective-permute-done((bf16[24,3840]{1,0:T(8,128)(2,1)S(1)}, bf16[24,3840]{1,0:T(8,128)(2,1)S(1)}, u32[]{:S(2)}, u32[]{:S(2)}) %collective-permute-start.41) | collective-permute-done | bytes 184352 | tf_op jit(solution)/shard_map/ppermute | solution.py:721
  (149 shorter events, 61.6 us)
Async XLA Ops:
  7.2 684.5 %reduce-scatter.4.cloned.1.call-start = ((), (), s32[]{:S(2)}) async-start(), calls=%async_computation.1 | async-start | bytes 5068800
  9.8 19.2 %collective-permute-start.7 = (bf16[24,2432]{1,0:T(8,128)(2,1)}, bf16[24,2432]{1,0:T(8,128)(2,1)}, u32[]{:S(2)}, u32[]{:S(2)}) collective-permute-start(bf16[24,2432]{1,0:T(8,128)(2,1)} %get-tuple-element.83), channel_id=1, source_target_pairs={{0,2},{1,3},{2,0},{3,1},{4,6},{5,7},{6,4},{7,5},{8,10},{9,11},{10,... | collective-permute-start | bytes 350216 | tf_op jit(solution)/shard_map/ppermute | solution.py:721
  13.9 15.8 %collective-permute-start.8 = (bf16[24,2432]{1,0:T(8,128)(2,1)}, bf16[24,2432]{1,0:T(8,128)(2,1)}, u32[]{:S(2)}, u32[]{:S(2)}) collective-permute-start(bf16[24,2432]{1,0:T(8,128)(2,1)} %get-tuple-element.83), channel_id=1, source_target_pairs={{0,3},{1,2},{2,1},{3,0},{4,7},{5,6},{6,5},{7,4},{8,11},{9,10},{10,... | collective-permute-start | bytes 350216 | tf_op jit(solution)/shard_map/ppermute | solution.py:721
  18.3 60.7 %collective-permute-start = (bf16[2,256,768]{2,1,0:T(8,128)(2,1)}, bf16[2,256,768]{2,1,0:T(8,128)(2,1)}, u32[]{:S(2)}, u32[]{:S(2)}) collective-permute-start(bf16[2,256,768]{2,1,0:T(8,128)(2,1)} %gather_fusion.2), channel_id=1, source_target_pairs={{0,1},{1,0},{2,3},{3,2},{4,5},{5,4},{6,7},{7,6},{8,9},{9,8},{10,11... | collective-permute-start | bytes 2359304 | tf_op jit(solution)/shard_map/ppermute | solution.py:721
  20.0 59.9 %collective-permute-start.1 = (bf16[2,256,768]{2,1,0:T(8,128)(2,1)}, bf16[2,256,768]{2,1,0:T(8,128)(2,1)}, u32[]{:S(2)}, u32[]{:S(2)}) collective-permute-start(bf16[2,256,768]{2,1,0:T(8,128)(2,1)} %gather_fusion.3), channel_id=1, source_target_pairs={{0,2},{1,3},{2,0},{3,1},{4,6},{5,7},{6,4},{7,5},{8,10},{9,11},{10,... | collective-permute-start | bytes 2359304 | tf_op jit(solution)/shard_map/ppermute | solution.py:721
  24.3 57.1 %collective-permute-start.2 = (bf16[2,256,768]{2,1,0:T(8,128)(2,1)}, bf16[2,256,768]{2,1,0:T(8,128)(2,1)}, u32[]{:S(2)}, u32[]{:S(2)}) collective-permute-start(bf16[2,256,768]{2,1,0:T(8,128)(2,1)} %gather_fusion.4), channel_id=1, source_target_pairs={{0,3},{1,2},{2,1},{3,0},{4,7},{5,6},{6,5},{7,4},{8,11},{9,10},{10,... | collective-permute-start | bytes 2359304 | tf_op jit(solution)/shard_map/ppermute | solution.py:721
  29.0 46.0 %collective-permute-start.6 = (bf16[24,2432]{1,0:T(8,128)(2,1)}, bf16[24,2432]{1,0:T(8,128)(2,1)S(1)}, u32[]{:S(2)}, u32[]{:S(2)}) collective-permute-start(bf16[24,2432]{1,0:T(8,128)(2,1)} %get-tuple-element.83), channel_id=1, source_target_pairs={{0,1},{1,0},{2,3},{3,2},{4,5},{5,4},{6,7},{7,6},{8,9},{9,8},{10,11... | collective-permute-start | bytes 350216 | tf_op jit(solution)/shard_map/ppermute | solution.py:721
  29.7 59.6 %collective-permute-start.13 = (bf16[24,6912]{1,0:T(8,128)(2,1)S(1)}, bf16[24,6912]{1,0:T(8,128)(2,1)}, u32[]{:S(2)}, u32[]{:S(2)}) collective-permute-start(bf16[24,6912]{1,0:T(8,128)(2,1)S(1)} %constant_dynamic-update-slice_fusion), channel_id=1, source_target_pairs={{0,1},{1,0},{2,3},{3,2},{4,5},{5,4},{6,7},{7,6},{8,9},{9,8},{10,11... | collective-permute-start | bytes 995336 | tf_op jit(solution)/shard_map/ppermute | solution.py:721
  75.0 39.6 %collective-permute-start.14 = (bf16[24,6912]{1,0:T(8,128)(2,1)S(1)}, bf16[24,6912]{1,0:T(8,128)(2,1)}, u32[]{:S(2)}, u32[]{:S(2)}) collective-permute-start(bf16[24,6912]{1,0:T(8,128)(2,1)S(1)} %constant_dynamic-update-slice_fusion), channel_id=1, source_target_pairs={{0,2},{1,3},{2,0},{3,1},{4,6},{5,7},{6,4},{7,5},{8,10},{9,11},{10,... | collective-permute-start | bytes 995336 | tf_op jit(solution)/shard_map/ppermute | solution.py:721
  79.0 38.7 %collective-permute-start.15 = (bf16[24,6912]{1,0:T(8,128)(2,1)S(1)}, bf16[24,6912]{1,0:T(8,128)(2,1)}, u32[]{:S(2)}, u32[]{:S(2)}) collective-permute-start(bf16[24,6912]{1,0:T(8,128)(2,1)S(1)} %constant_dynamic-update-slice_fusion), channel_id=1, source_target_pairs={{0,3},{1,2},{2,1},{3,0},{4,7},{5,6},{6,5},{7,4},{8,11},{9,10},{10,... | collective-permute-start | bytes 995336 | tf_op jit(solution)/shard_map/ppermute | solution.py:721
  79.9 48.5 %collective-permute-start.9 = (bf16[4,24,2432]{2,1,0:T(8,128)(2,1)}, bf16[4,24,2432]{2,1,0:T(8,128)(2,1)}, u32[]{:S(2)}, u32[]{:S(2)}) collective-permute-start(bf16[4,24,2432]{2,1,0:T(8,128)(2,1)} %get-tuple-element.81), channel_id=1, source_target_pairs={{0,8},{4,12},{8,0},{12,4},{16,24},{20,28},{24,16},{28,20},{1,9},{5... | collective-permute-start | bytes 1400840 | tf_op jit(solution)/shard_map/ppermute | solution.py:721
  81.4 48.5 %collective-permute-start.10 = (bf16[4,24,2432]{2,1,0:T(8,128)(2,1)}, bf16[4,24,2432]{2,1,0:T(8,128)(2,1)}, u32[]{:S(2)}, u32[]{:S(2)}) collective-permute-start(bf16[4,24,2432]{2,1,0:T(8,128)(2,1)} %get-tuple-element.81), channel_id=1, source_target_pairs={{0,16},{4,20},{8,24},{12,28},{16,0},{20,4},{24,8},{28,12},{1,17},{... | collective-permute-start | bytes 1400840 | tf_op jit(solution)/shard_map/ppermute | solution.py:721
  89.3 42.0 %collective-permute-start.11 = (bf16[4,24,2432]{2,1,0:T(8,128)(2,1)}, bf16[4,24,2432]{2,1,0:T(8,128)(2,1)}, u32[]{:S(2)}, u32[]{:S(2)}) collective-permute-start(bf16[4,24,2432]{2,1,0:T(8,128)(2,1)} %get-tuple-element.81), channel_id=1, source_target_pairs={{0,24},{4,28},{8,16},{12,20},{16,8},{20,12},{24,0},{28,4},{1,25},{... | collective-permute-start | bytes 1400840 | tf_op jit(solution)/shard_map/ppermute | solution.py:721
  114.6 32.4 %collective-permute-start.3 = (bf16[2,256,768]{2,1,0:T(8,128)(2,1)}, bf16[2,256,768]{2,1,0:T(8,128)(2,1)}, u32[]{:S(2)}, u32[]{:S(2)}) collective-permute-start(bf16[2,256,768]{2,1,0:T(8,128)(2,1)} %gather_fusion.6), channel_id=1, source_target_pairs={{0,1},{1,0},{2,3},{3,2},{4,5},{5,4},{6,7},{7,6},{8,9},{9,8},{10,11... | collective-permute-start | bytes 2359304 | tf_op jit(solution)/shard_map/ppermute | solution.py:721
  117.7 58.3 %collective-permute-start.4 = (bf16[2,256,768]{2,1,0:T(8,128)(2,1)}, bf16[2,256,768]{2,1,0:T(8,128)(2,1)}, u32[]{:S(2)}, u32[]{:S(2)}) collective-permute-start(bf16[2,256,768]{2,1,0:T(8,128)(2,1)} %gather_fusion.7), channel_id=1, source_target_pairs={{0,2},{1,3},{2,0},{3,1},{4,6},{5,7},{6,4},{7,5},{8,10},{9,11},{10,... | collective-permute-start | bytes 2359304 | tf_op jit(solution)/shard_map/ppermute | solution.py:721
  123.5 26.9 %copy-start.4 = (bf16[1,4,24,2432]{3,2,1,0:T(8,128)(2,1)S(1)}, bf16[1,4,24,2432]{3,2,1,0:T(8,128)(2,1)}, u32[]{:S(2)}) copy-start(bf16[1,4,24,2432]{3,2,1,0:T(8,128)(2,1)} %get-tuple-element.80) | copy-start | bytes 1400836
  128.3 55.7 %collective-permute-start.16 = (bf16[4,24,6912]{2,1,0:T(8,128)(2,1)S(1)}, bf16[4,24,6912]{2,1,0:T(8,128)(2,1)}, u32[]{:S(2)}, u32[]{:S(2)}) collective-permute-start(bf16[4,24,6912]{2,1,0:T(8,128)(2,1)S(1)} %get-tuple-element.73), channel_id=1, source_target_pairs={{0,8},{4,12},{8,0},{12,4},{16,24},{20,28},{24,16},{28,20},{1,9},{5... | collective-permute-start | bytes 3981320 | tf_op jit(solution)/shard_map/ppermute | solution.py:721
  129.8 59.0 %collective-permute-start.17 = (bf16[4,24,6912]{2,1,0:T(8,128)(2,1)S(1)}, bf16[4,24,6912]{2,1,0:T(8,128)(2,1)}, u32[]{:S(2)}, u32[]{:S(2)}) collective-permute-start(bf16[4,24,6912]{2,1,0:T(8,128)(2,1)S(1)} %get-tuple-element.73), channel_id=1, source_target_pairs={{0,16},{4,20},{8,24},{12,28},{16,0},{20,4},{24,8},{28,12},{1,17},{... | collective-permute-start | bytes 3981320 | tf_op jit(solution)/shard_map/ppermute | solution.py:721
  131.4 57.5 %collective-permute-start.18 = (bf16[4,24,6912]{2,1,0:T(8,128)(2,1)S(1)}, bf16[4,24,6912]{2,1,0:T(8,128)(2,1)}, u32[]{:S(2)}, u32[]{:S(2)}) collective-permute-start(bf16[4,24,6912]{2,1,0:T(8,128)(2,1)S(1)} %get-tuple-element.73), channel_id=1, source_target_pairs={{0,24},{4,28},{8,16},{12,20},{16,8},{20,12},{24,0},{28,4},{1,25},{... | collective-permute-start | bytes 3981320 | tf_op jit(solution)/shard_map/ppermute | solution.py:721
  146.9 33.6 %collective-permute-start.5 = (bf16[2,256,768]{2,1,0:T(8,128)(2,1)}, bf16[2,256,768]{2,1,0:T(8,128)(2,1)}, u32[]{:S(2)}, u32[]{:S(2)}) collective-permute-start(bf16[2,256,768]{2,1,0:T(8,128)(2,1)} %gather_fusion.8), channel_id=1, source_target_pairs={{0,3},{1,2},{2,1},{3,0},{4,7},{5,6},{6,5},{7,4},{8,11},{9,10},{10,... | collective-permute-start | bytes 2359304 | tf_op jit(solution)/shard_map/ppermute | solution.py:721
  150.4 26.1 %copy-start.16 = (s32[1,8]{1,0:T(1,128)S(1)}, s32[1,8]{1,0:T(1,128)}, u32[]{:S(2)}) copy-start(s32[1,8]{1,0:T(1,128)} %param.14) | copy-start | bytes 100
  176.0 18.2 %collective-permute-start.12 = (bf16[16,24,2432]{2,1,0:T(8,128)(2,1)}, bf16[16,24,2432]{2,1,0:T(8,128)(2,1)}, u32[]{:S(2)}, u32[]{:S(2)}) collective-permute-start(bf16[16,24,2432]{2,1,0:T(8,128)(2,1)} %bitcast.16.refs_0_), channel_id=1, source_target_pairs={{0,4},{4,0},{8,12},{12,8},{16,20},{20,16},{24,28},{28,24},{1,5},{5... | collective-permute-start | bytes 5603336 | tf_op jit(solution)/shard_map/ppermute | solution.py:721
  194.1 35.9 %collective-permute-start.19 = (bf16[16,24,6912]{2,1,0:T(8,128)(2,1)}, bf16[16,24,6912]{2,1,0:T(8,128)(2,1)}, u32[]{:S(2)}, u32[]{:S(2)}) collective-permute-start(bf16[16,24,6912]{2,1,0:T(8,128)(2,1)} %bitcast.28.refs_0_), channel_id=1, source_target_pairs={{0,4},{4,0},{8,12},{12,8},{16,20},{20,16},{24,28},{28,24},{1,5},{5... | collective-permute-start | bytes 15925256 | tf_op jit(solution)/shard_map/ppermute | solution.py:721
  328.8 276.2 %collective-permute-start.36 = (bf16[4,96,3840]{2,1,0:T(8,128)(2,1)}, bf16[4,96,3840]{2,1,0:T(8,128)(2,1)}, u32[]{:S(2)}, u32[]{:S(2)}) collective-permute-start(bf16[4,96,3840]{2,1,0:T(8,128)(2,1)} %dynamic-slice_bitcast_fusion), channel_id=1, source_target_pairs={{0,4},{4,0},{8,12},{12,8},{16,20},{20,16},{24,28},{28,24},{1,5},{5... | collective-permute-start | bytes 8847368 | tf_op jit(solution)/shard_map/ppermute | solution.py:721
  398.0 76.3 %collective-permute-start.26 = (bf16[1,256,768]{2,1,0:T(8,128)(2,1)S(1)}, bf16[1,256,768]{2,1,0:T(8,128)(2,1)S(1)}, u32[]{:S(2)}, u32[]{:S(2)}) collective-permute-start(bf16[1,256,768]{2,1,0:T(8,128)(2,1)S(1)} %get-tuple-element.66), channel_id=1, source_target_pairs={{0,1},{1,0},{2,3},{3,2},{4,5},{5,4},{6,7},{7,6},{8,9},{9,8},{10,11... | collective-permute-start | bytes 1179656 | tf_op jit(solution)/shard_map/ppermute | solution.py:721
  447.9 33.7 %collective-permute-start.27 = (bf16[1,256,768]{2,1,0:T(8,128)(2,1)S(1)}, bf16[1,256,768]{2,1,0:T(8,128)(2,1)S(1)}, u32[]{:S(2)}, u32[]{:S(2)}) collective-permute-start(bf16[1,256,768]{2,1,0:T(8,128)(2,1)S(1)} %get-tuple-element.65), channel_id=1, source_target_pairs={{0,2},{1,3},{2,0},{3,1},{4,6},{5,7},{6,4},{7,5},{8,10},{9,11},{10,... | collective-permute-start | bytes 1179656 | tf_op jit(solution)/shard_map/ppermute | solution.py:721
  470.2 17.9 %collective-permute-start.28 = (bf16[1,256,768]{2,1,0:T(8,128)(2,1)S(1)}, bf16[1,256,768]{2,1,0:T(8,128)(2,1)S(1)}, u32[]{:S(2)}, u32[]{:S(2)}) collective-permute-start(bf16[1,256,768]{2,1,0:T(8,128)(2,1)S(1)} %get-tuple-element.64), channel_id=1, source_target_pairs={{0,3},{1,2},{2,1},{3,0},{4,7},{5,6},{6,5},{7,4},{8,11},{9,10},{10,... | collective-permute-start | bytes 1179656 | tf_op jit(solution)/shard_map/ppermute | solution.py:721
  473.3 122.1 %collective-permute-start.29 = (bf16[4,96,2432]{2,1,0:T(8,128)(2,1)}, bf16[4,96,2432]{2,1,0:T(8,128)(2,1)}, u32[]{:S(2)}, u32[]{:S(2)}) collective-permute-start(bf16[4,96,2432]{2,1,0:T(8,128)(2,1)} %dynamic-slice_bitcast_fusion.1), channel_id=1, source_target_pairs={{0,4},{4,0},{8,12},{12,8},{16,20},{20,16},{24,28},{28,24},{1,5},{5... | collective-permute-start | bytes 5603336 | tf_op jit(solution)/shard_map/ppermute | solution.py:721
  474.3 20.1 %collective-permute-start.23 = (bf16[1,256,768]{2,1,0:T(8,128)(2,1)}, bf16[1,256,768]{2,1,0:T(8,128)(2,1)}, u32[]{:S(2)}, u32[]{:S(2)}) collective-permute-start(bf16[1,256,768]{2,1,0:T(8,128)(2,1)} %get-tuple-element.70), channel_id=1, source_target_pairs={{0,1},{1,0},{2,3},{3,2},{4,5},{5,4},{6,7},{7,6},{8,9},{9,8},{10,11... | collective-permute-start | bytes 1179656 | tf_op jit(solution)/shard_map/ppermute | solution.py:721
  481.6 40.6 %collective-permute-start.24 = (bf16[1,256,768]{2,1,0:T(8,128)(2,1)}, bf16[1,256,768]{2,1,0:T(8,128)(2,1)}, u32[]{:S(2)}, u32[]{:S(2)}) collective-permute-start(bf16[1,256,768]{2,1,0:T(8,128)(2,1)} %get-tuple-element.69), channel_id=1, source_target_pairs={{0,2},{1,3},{2,0},{3,1},{4,6},{5,7},{6,4},{7,5},{8,10},{9,11},{10,... | collective-permute-start | bytes 1179656 | tf_op jit(solution)/shard_map/ppermute | solution.py:721
  488.1 34.2 %collective-permute-start.25 = (bf16[1,256,768]{2,1,0:T(8,128)(2,1)S(1)}, bf16[1,256,768]{2,1,0:T(8,128)(2,1)}, u32[]{:S(2)}, u32[]{:S(2)}) collective-permute-start(bf16[1,256,768]{2,1,0:T(8,128)(2,1)S(1)} %get-tuple-element.68), channel_id=1, source_target_pairs={{0,3},{1,2},{2,1},{3,0},{4,7},{5,6},{6,5},{7,4},{8,11},{9,10},{10,... | collective-permute-start | bytes 1179656 | tf_op jit(solution)/shard_map/ppermute | solution.py:721
  490.8 40.6 %copy-start.9 = (s32[8]{0:T(128)S(1)}, s32[8]{0:T(128)}, u32[]{:S(2)}) copy-start(s32[8]{0:T(128)} %copy-done.8) | copy-start | bytes 100
  494.4 41.5 %collective-permute-start.20 = (bf16[2,256,768]{2,1,0:T(8,128)(2,1)}, bf16[2,256,768]{2,1,0:T(8,128)(2,1)S(1)}, u32[]{:S(2)}, u32[]{:S(2)}) collective-permute-start(bf16[2,256,768]{2,1,0:T(8,128)(2,1)} %get-tuple-element.62), channel_id=1, source_target_pairs={{0,1},{1,0},{2,3},{3,2},{4,5},{5,4},{6,7},{7,6},{8,9},{9,8},{10,11... | collective-permute-start | bytes 2359304 | tf_op jit(solution)/shard_map/ppermute | solution.py:721
  522.3 68.5 %collective-permute-start.21 = (bf16[2,256,768]{2,1,0:T(8,128)(2,1)}, bf16[2,256,768]{2,1,0:T(8,128)(2,1)S(1)}, u32[]{:S(2)}, u32[]{:S(2)}) collective-permute-start(bf16[2,256,768]{2,1,0:T(8,128)(2,1)} %get-tuple-element.61), channel_id=1, source_target_pairs={{0,2},{1,3},{2,0},{3,1},{4,6},{5,7},{6,4},{7,5},{8,10},{9,11},{10,... | collective-permute-start | bytes 2359304 | tf_op jit(solution)/shard_map/ppermute | solution.py:721
  522.3 68.5 %collective-permute-start.22 = (bf16[2,256,768]{2,1,0:T(8,128)(2,1)}, bf16[2,256,768]{2,1,0:T(8,128)(2,1)S(1)}, u32[]{:S(2)}, u32[]{:S(2)}) collective-permute-start(bf16[2,256,768]{2,1,0:T(8,128)(2,1)} %get-tuple-element.60), channel_id=1, source_target_pairs={{0,3},{1,2},{2,1},{3,0},{4,7},{5,6},{6,5},{7,4},{8,11},{9,10},{10,... | collective-permute-start | bytes 2359304 | tf_op jit(solution)/shard_map/ppermute | solution.py:721
  535.9 54.9 %copy-start.10 = (bf16[2,256,768]{2,1,0:T(8,128)(2,1)}, bf16[2,256,768]{2,1,0:T(8,128)(2,1)S(1)}, u32[]{:S(2)}) copy-start(bf16[2,256,768]{2,1,0:T(8,128)(2,1)S(1)} %collective-permute-done.20.refs_1_) | copy-start | bytes 2359300
  597.5 17.6 %collective-permute-start.30 = (bf16[96,2432]{1,0:T(8,128)(2,1)S(1)}, bf16[96,2432]{1,0:T(8,128)(2,1)S(1)}, u32[]{:S(2)}, u32[]{:S(2)}) collective-permute-start(bf16[96,2432]{1,0:T(8,128)(2,1)S(1)} %get-tuple-element.57), channel_id=1, source_target_pairs={{0,8},{4,12},{8,0},{12,4},{16,24},{20,28},{24,16},{28,20},{1,9},{5... | collective-permute-start | bytes 1400840 | tf_op jit(solution)/shard_map/ppermute | solution.py:721
  603.5 24.3 %collective-permute-start.31 = (bf16[96,2432]{1,0:T(8,128)(2,1)S(1)}, bf16[96,2432]{1,0:T(8,128)(2,1)S(1)}, u32[]{:S(2)}, u32[]{:S(2)}) collective-permute-start(bf16[96,2432]{1,0:T(8,128)(2,1)S(1)} %get-tuple-element.59), channel_id=1, source_target_pairs={{0,16},{4,20},{8,24},{12,28},{16,0},{20,4},{24,8},{28,12},{1,17},{... | collective-permute-start | bytes 1400840 | tf_op jit(solution)/shard_map/ppermute | solution.py:721
  603.5 24.3 %collective-permute-start.32 = (bf16[96,2432]{1,0:T(8,128)(2,1)S(1)}, bf16[96,2432]{1,0:T(8,128)(2,1)S(1)}, u32[]{:S(2)}, u32[]{:S(2)}) collective-permute-start(bf16[96,2432]{1,0:T(8,128)(2,1)S(1)} %get-tuple-element.58), channel_id=1, source_target_pairs={{0,24},{4,28},{8,16},{12,20},{16,8},{20,12},{24,0},{28,4},{1,25},{... | collective-permute-start | bytes 1400840 | tf_op jit(solution)/shard_map/ppermute | solution.py:721
  607.8 44.6 %collective-permute-start.37 = (bf16[96,3840]{1,0:T(8,128)(2,1)S(1)}, bf16[96,3840]{1,0:T(8,128)(2,1)S(1)}, u32[]{:S(2)}, u32[]{:S(2)}) collective-permute-start(bf16[96,3840]{1,0:T(8,128)(2,1)S(1)} %get-tuple-element.54), channel_id=1, source_target_pairs={{0,8},{4,12},{8,0},{12,4},{16,24},{20,28},{24,16},{28,20},{1,9},{5... | collective-permute-start | bytes 2211848 | tf_op jit(solution)/shard_map/ppermute | solution.py:721
  609.8 43.9 %collective-permute-start.38 = (bf16[96,3840]{1,0:T(8,128)(2,1)S(1)}, bf16[96,3840]{1,0:T(8,128)(2,1)S(1)}, u32[]{:S(2)}, u32[]{:S(2)}) collective-permute-start(bf16[96,3840]{1,0:T(8,128)(2,1)S(1)} %get-tuple-element.56), channel_id=1, source_target_pairs={{0,16},{4,20},{8,24},{12,28},{16,0},{20,4},{24,8},{28,12},{1,17},{... | collective-permute-start | bytes 2211848 | tf_op jit(solution)/shard_map/ppermute | solution.py:721
  615.0 38.7 %collective-permute-start.39 = (bf16[96,3840]{1,0:T(8,128)(2,1)S(1)}, bf16[96,3840]{1,0:T(8,128)(2,1)S(1)}, u32[]{:S(2)}, u32[]{:S(2)}) collective-permute-start(bf16[96,3840]{1,0:T(8,128)(2,1)S(1)} %get-tuple-element.55), channel_id=1, source_target_pairs={{0,24},{4,28},{8,16},{12,20},{16,8},{20,12},{24,0},{28,4},{1,25},{... | collective-permute-start | bytes 2211848 | tf_op jit(solution)/shard_map/ppermute | solution.py:721
  629.4 45.9 %collective-permute-start.33 = (bf16[24,2432]{1,0:T(8,128)(2,1)S(1)}, bf16[24,2432]{1,0:T(8,128)(2,1)S(1)}, u32[]{:S(2)}, u32[]{:S(2)}) collective-permute-start(bf16[24,2432]{1,0:T(8,128)(2,1)S(1)} %get-tuple-element.77), channel_id=1, source_target_pairs={{0,1},{1,0},{2,3},{3,2},{4,5},{5,4},{6,7},{7,6},{8,9},{9,8},{10,11... | collective-permute-start | bytes 350216 | tf_op jit(solution)/shard_map/ppermute | solution.py:721
  647.4 30.3 %collective-permute-start.34 = (bf16[24,2432]{1,0:T(8,128)(2,1)S(1)}, bf16[24,2432]{1,0:T(8,128)(2,1)S(1)}, u32[]{:S(2)}, u32[]{:S(2)}) collective-permute-start(bf16[24,2432]{1,0:T(8,128)(2,1)S(1)} %get-tuple-element.79), channel_id=1, source_target_pairs={{0,2},{1,3},{2,0},{3,1},{4,6},{5,7},{6,4},{7,5},{8,10},{9,11},{10,... | collective-permute-start | bytes 350216 | tf_op jit(solution)/shard_map/ppermute | solution.py:721
  652.4 25.3 %collective-permute-start.35 = (bf16[24,2432]{1,0:T(8,128)(2,1)S(1)}, bf16[24,2432]{1,0:T(8,128)(2,1)S(1)}, u32[]{:S(2)}, u32[]{:S(2)}) collective-permute-start(bf16[24,2432]{1,0:T(8,128)(2,1)S(1)} %get-tuple-element.78), channel_id=1, source_target_pairs={{0,3},{1,2},{2,1},{3,0},{4,7},{5,6},{6,5},{7,4},{8,11},{9,10},{10,... | collective-permute-start | bytes 350216 | tf_op jit(solution)/shard_map/ppermute | solution.py:721
  655.7 24.7 %collective-permute-start.40 = (bf16[24,3840]{1,0:T(8,128)(2,1)S(1)}, bf16[24,3840]{1,0:T(8,128)(2,1)S(1)}, u32[]{:S(2)}, u32[]{:S(2)}) collective-permute-start(bf16[24,3840]{1,0:T(8,128)(2,1)S(1)} %get-tuple-element.74), channel_id=1, source_target_pairs={{0,1},{1,0},{2,3},{3,2},{4,5},{5,4},{6,7},{7,6},{8,9},{9,8},{10,11... | collective-permute-start | bytes 552968 | tf_op jit(solution)/shard_map/ppermute | solution.py:721
  675.2 15.0 %collective-permute-start.41 = (bf16[24,3840]{1,0:T(8,128)(2,1)S(1)}, bf16[24,3840]{1,0:T(8,128)(2,1)S(1)}, u32[]{:S(2)}, u32[]{:S(2)}) collective-permute-start(bf16[24,3840]{1,0:T(8,128)(2,1)S(1)} %get-tuple-element.76), channel_id=1, source_target_pairs={{0,2},{1,3},{2,0},{3,1},{4,6},{5,7},{6,4},{7,5},{8,10},{9,11},{10,... | collective-permute-start | bytes 552968 | tf_op jit(solution)/shard_map/ppermute | solution.py:721
  675.2 15.0 %collective-permute-start.42 = (bf16[24,3840]{1,0:T(8,128)(2,1)S(1)}, bf16[24,3840]{1,0:T(8,128)(2,1)S(1)}, u32[]{:S(2)}, u32[]{:S(2)}) collective-permute-start(bf16[24,3840]{1,0:T(8,128)(2,1)S(1)} %get-tuple-element.75), channel_id=1, source_target_pairs={{0,3},{1,2},{2,1},{3,0},{4,7},{5,6},{6,5},{7,4},{8,11},{9,10},{10,... | collective-permute-start | bytes 552968 | tf_op jit(solution)/shard_map/ppermute | solution.py:721
  (13 other events, 86.4 us)
Sparse Core Ops, SparseCore 0:
  489.0 148.0 reduce-scatter.3
where the time goes:
time: 709 us; the launch traced here: 705 us
  waiting for transfers between devices  215 us (30%)
  Pallas kernels  210 us (30%)
  starting transfers between devices  195 us (28%)
  local copies, waits for them, and re-layouts  45.9 us (6%)
  other arithmetic  23.8 us (3%)
  between operations  14.6 us (2%)
    ppermute x43, waiting for transfers between devices, swap(): return lax.ppermute(x, axis, [(s, s ^ bits) for s in range(size)])  215 us
    ppermute x43, starting transfers between devices, swap(): return lax.ppermute(x, axis, [(s, s ^ bits) for s in range(size)])  195 us
    pallas_call x2, Pallas kernels, attn_bwd(): pl.pallas_call(functools.partial(attn_bwd_kernel, m=m, begin=begin), grid...  66.5 us
    pallas_call x1, Pallas kernels, mlp_bwd(): pl.pallas_call(functools.partial(mlp_bwd_kernel, share=share), grid_spec=...  60 us
    pallas_call x1, Pallas kernels, attn_fwd(): pl.pallas_call(attn_fwd_kernel, grid_spec=pltpu.PrefetchScalarGridSpec(nu...  29.4 us
    pallas_call x1, Pallas kernels, mlp_fwd(): pl.pallas_call(mlp_fwd_kernel, grid_spec=pltpu.PrefetchScalarGridSpec(num...  24.8 us
    gather x8, local copies, waits for them, and re-layouts, deal(): jnp.take(array, send_at[b * mb:(b + 1) * mb], axis=0, mode='clip')  15.6 us
    pallas_call x2, Pallas kernels, place_weights(): pl.pallas_call(kernel, grid_spec=pltpu.PrefetchScalarGridSpec(num_scalar_...  15 us
  transfers between devices with their start and end apart: 44, of which 14 were waited for; matrix products, arithmetic and copies ran while one was open for 8% of the time, Pallas kernels for 16%

commit v1 on v0

--- a/solution.py
+++ b/solution.py
@@ -14,6 +14,7 @@
 ROWS = 256
 HALF = 128
 GROUP = 3
+BACK_GROUP = 2
 BF = jnp.bfloat16
 F32 = jnp.float32
 ALPHA = 1.0 / math.sqrt(DEPTH)
@@ -276,10 +277,10 @@
     )(lens, low, x, vec, rest, wdown)
 
 
-def mlp_bwd_kernel(lens, low_ref, mid_ref, cot_ref, vec_ref, rest_ref, wd_ref,
-                   gmid_ref, gmix_ref, inner_ref, gmain_ref, gdown_ref,
+def mlp_bwd_kernel(lens, core, low_ref, mid_ref, cot_ref, vec_ref, rest_ref, wd_ref,
+                   gmid_ref, gmix_ref, inner_ref, keep_ref, give_ref, gdown_ref,
                    wout_ref, wup_ref, wdown_ref, aout_ref, aup_ref, adown_ref, gvec_ref, e2_ref,
-                   stage_ref, down_ref, sem, *, share):
+                   stage_ref, down_ref, sem, half_sem, *, share):
     m = pl.program_id(0)
     i = pl.program_id(1)
     d = mid_ref.shape[2]
@@ -360,8 +361,21 @@
         main = d + ff
         stage_ref[:, 0:d] = aout_ref[...].astype(BF)
         stage_ref[:, d:main] = aup_ref[...].astype(BF)
-        send = pltpu.make_async_copy(stage_ref, gmain_ref, sem.at[0])
-        send.start()
+        each = keep_ref.shape[1]
+
+        def halves(step):
+            for n in range(2 * keep_ref.shape[0]):
+                src = stage_ref.at[n * each:(n + 1) * each, :]
+
+                @pl.when(core[0] == n % 2)
+                def _():
+                    step(pltpu.make_async_copy(src, keep_ref.at[n // 2], half_sem.at[n]))
+
+                @pl.when(core[0] != n % 2)
+                def _():
+                    step(pltpu.make_async_copy(src, give_ref.at[n // 2], half_sem.at[n]))
+
+        halves(lambda c: c.start())
         if share % 8 == 0:
 
             def regroup(e, carry):
@@ -380,34 +394,35 @@
         down_ref[:, ff:ff + 128] = jnp.transpose(gvec_ref[...]).astype(BF)
         last = pltpu.make_async_copy(down_ref, gdown_ref, sem.at[1])
         last.start()
-        send.wait()
+        halves(lambda c: c.wait())
         last.wait()
 
 
-def mlp_bwd(lens, low, mid, cot, rest, wdown, vec, share):
+def mlp_bwd(lens, core, low, mid, cot, rest, wdown, vec, share, dp):
     mb, rows, d = mid.shape
     ff = wdown.shape[0]
 
-    def blk(m, i, ln):
+    def blk(m, i, ln, core):
         return (m, jnp.minimum(i, last_block(ln, m)), 0)
 
     return pl.pallas_call(
         functools.partial(mlp_bwd_kernel, share=share),
         grid_spec=pltpu.PrefetchScalarGridSpec(
-            num_scalar_prefetch=1,
+            num_scalar_prefetch=2,
             grid=(mb, rows // ROWS),
             in_specs=[
                 pl.BlockSpec((1, ROWS, d), blk),
                 pl.BlockSpec((1, ROWS, d), blk),
                 pl.BlockSpec((1, ROWS, d), blk),
-                pl.BlockSpec((8, d), lambda m, i, ln: (0, 0)),
+                pl.BlockSpec((8, d), lambda m, i, ln, core: (0, 0)),
                 pl.BlockSpec(memory_space=pl.ANY),
                 pl.BlockSpec(memory_space=pl.ANY),
             ],
             out_specs=[
                 pl.BlockSpec((1, ROWS, d), blk),
                 pl.BlockSpec((1, ROWS, d), blk),
-                pl.BlockSpec((1, 16, ROWS), lambda m, i, ln: (m, 0, jnp.minimum(i, last_block(ln, m)))),
+                pl.BlockSpec((1, 16, ROWS), lambda m, i, ln, core: (m, 0, jnp.minimum(i, last_block(ln, m)))),
+                pl.BlockSpec(memory_space=pl.ANY),
                 pl.BlockSpec(memory_space=pl.ANY),
                 pl.BlockSpec(memory_space=pl.ANY),
             ],
@@ -423,27 +438,29 @@
                 pltpu.VMEM((d, d + ff), BF),
                 pltpu.VMEM((d, ff + 128), BF),
                 pltpu.SemaphoreType.DMA((2 * (ff // d) + 1,)),
+                pltpu.SemaphoreType.DMA((dp,)),
             ],
         ),
         out_shape=[
             jax.ShapeDtypeStruct((mb, rows, d), F32),
             jax.ShapeDtypeStruct((mb, rows, d), BF),
             jax.ShapeDtypeStruct((mb, 16, rows), F32),
-            jax.ShapeDtypeStruct((d, d + ff), BF),
+            jax.ShapeDtypeStruct((dp // 2, d // dp, d + ff), BF),
+            jax.ShapeDtypeStruct((dp // 2, d // dp, d + ff), BF),
             jax.ShapeDtypeStruct((d, ff + 128), BF),
         ],
         compiler_params=params(2),
         cost_estimate=cost(80, 60 << 20),
         name="mlp_bwd",
-    )(lens, low, mid, cot, vec, rest, wdown)
-
-
-def attn_bwd_kernel(lens, x_ref, q_ref, k_ref, v_ref, gmix_ref, gmid_ref, lse_ref, inner_ref,
+    )(lens, core, low, mid, cot, vec, rest, wdown)
+
+
+def attn_bwd_kernel(lens, core, x_ref, q_ref, k_ref, v_ref, gmix_ref, gmid_ref, lse_ref, inner_ref,
                     w_ref, vec_ref, *rest, m, begin):
     if begin:
         dx_ref, gw_ref, acc_ref, gvec_ref, dk_ref, dv_ref, gq_ref = rest
     else:
-        prev_ref, dx_ref, gw_ref, acc_ref, gvec_ref, dk_ref, dv_ref, gq_ref, before_ref, sem = rest
+        prev_ref, dx_ref, keep_ref, give_ref, acc_ref, gvec_ref, dk_ref, dv_ref, gq_ref, before_ref, sem = rest
     g = pl.program_id(0)
     i = pl.num_programs(0) - 1 - g
     d = x_ref.shape[2]
@@ -476,8 +493,8 @@
 
             def group(gp, carry):
                 spans, keep = [], []
-                for sub in range(GROUP):
-                    hp = gp * GROUP + sub
+                for sub in range(BACK_GROUP):
+                    hp = gp * BACK_GROUP + sub
                     span = pl.ds(pl.multiple_of(hp * 128, 128), 128)
                     spans.append(span)
                     q = q_ref[0, 0:size, span].astype(F32) * 0.125
@@ -490,7 +507,7 @@
                         gh = jnp.where(mine, gm, jnp.zeros_like(gm))
                         keep.append((hp * 2 + h, qh, gh, dot(k, qh, 1, 1), dot(v, gh, 1, 1)))
                 results = []
-                for sub in range(GROUP):
+                for sub in range(BACK_GROUP):
                     k_t = jnp.transpose(k_ref[0, 0:keys, spans[sub]])
                     probs, grads, dqs = [], [], []
                     for h in range(2):
@@ -513,7 +530,7 @@
                     dk_ref[0:keys, span] = jnp.where(fresh, 0.0, dk_ref[0:keys, span]) + dk
                 return carry
 
-            lax.fori_loop(0, d // (128 * GROUP), group, 0)
+            lax.fori_loop(0, d // (128 * BACK_GROUP), group, 0)
 
     for ii in range(x_rows_blocks(dk_ref)):
         variant(ii, ROWS)
@@ -548,43 +565,57 @@
 
     @pl.when(i == 0)
     def _():
-        total = acc_ref[...]
         rows = jnp.transpose(gvec_ref[...])
-        if not begin:
+        if begin:
+            gw_ref[:, 0:3 * d] = acc_ref[...].astype(BF)
+            gw_ref[:, 3 * d:] = rows.astype(BF)
+        else:
             pltpu.make_async_copy(prev_ref, before_ref, sem).wait()
-            total = total + before_ref[:, 0:3 * d].astype(F32)
-            rows = rows + before_ref[:, 3 * d:].astype(F32)
-        gw_ref[:, 0:3 * d] = total.astype(BF)
-        gw_ref[:, 3 * d:] = rows.astype(BF)
-
-
-def attn_bwd(m, prev, lens, x, qkv, gmix, gmid, lse, inner, gathered, vec):
+            each = keep_ref.shape[1]
+            for n in range(2 * keep_ref.shape[0]):
+                at = slice(n * each, (n + 1) * each)
+                wide = (acc_ref[at, :] + before_ref[at, 0:3 * d].astype(F32)).astype(BF)
+                thin = (rows[at] + before_ref[at, 3 * d:].astype(F32)).astype(BF)
+
+                @pl.when(core[0] == n % 2)
+                def _():
+                    keep_ref[n // 2, :, 0:3 * d] = wide
+                    keep_ref[n // 2, :, 3 * d:] = thin
+
+                @pl.when(core[0] != n % 2)
+                def _():
+                    give_ref[n // 2, :, 0:3 * d] = wide
+                    give_ref[n // 2, :, 3 * d:] = thin
+
+
+def attn_bwd(m, prev, dp, lens, core, x, qkv, gmix, gmid, lse, inner, gathered, vec):
     _, rows, d = x.shape
     nb = rows // ROWS
     begin = m == 0
 
-    def blk(g, ln):
+    def blk(g, ln, core):
         return (m, jnp.minimum(nb - 1 - g, last_block(ln, m)), 0)
 
-    def stat(g, ln):
+    def stat(g, ln, core):
         return (m, 0, jnp.minimum(nb - 1 - g, last_block(ln, m)))
 
-    def fixed(g, ln):
+    def fixed(g, ln, core):
         return (0, 0)
 
     one = pl.Buffered(1)
     whole = (d, 3 * d)
     wide = (d, 3 * d + 128)
+    split = (dp // 2, d // dp, 3 * d + 128)
     return pl.pallas_call(
         functools.partial(attn_bwd_kernel, m=m, begin=begin),
         grid_spec=pltpu.PrefetchScalarGridSpec(
-            num_scalar_prefetch=1,
+            num_scalar_prefetch=2,
             grid=(nb,),
             in_specs=[
                 pl.BlockSpec((1, ROWS, d), blk),
                 pl.BlockSpec((1, ROWS, d), blk),
-                pl.BlockSpec((1, rows, d), lambda g, ln: (m, 0, 1), pipeline_mode=one),
-                pl.BlockSpec((1, rows, d), lambda g, ln: (m, 0, 2), pipeline_mode=one),
+                pl.BlockSpec((1, rows, d), lambda g, ln, core: (m, 0, 1), pipeline_mode=one),
+                pl.BlockSpec((1, rows, d), lambda g, ln, core: (m, 0, 2), pipeline_mode=one),
                 pl.BlockSpec((1, ROWS, d), blk),
                 pl.BlockSpec((1, ROWS, d), blk),
                 pl.BlockSpec((1, 16, ROWS), stat),
@@ -593,9 +624,9 @@
                 pl.BlockSpec((8, d), fixed),
             ] + ([] if begin else [pl.BlockSpec(memory_space=pl.ANY)]),
             out_specs=[
-                pl.BlockSpec((1, ROWS, d), lambda g, ln: (0, nb - 1 - g, 0)),
-                pl.BlockSpec(wide, fixed, pipeline_mode=one),
-            ],
+                pl.BlockSpec((1, ROWS, d), lambda g, ln, core: (0, nb - 1 - g, 0)),
+            ] + ([pl.BlockSpec(wide, fixed, pipeline_mode=one)] if begin else [
+                pl.BlockSpec(split, lambda g, ln, core: (0, 0, 0), pipeline_mode=one)] * 2),
             scratch_shapes=[
                 pltpu.VMEM(whole, F32),
                 pltpu.VMEM((128, d), F32),
@@ -604,11 +635,12 @@
                 pltpu.VMEM((ROWS, 3 * d), BF),
             ] + ([] if begin else [pltpu.VMEM(wide, BF), pltpu.SemaphoreType.DMA(())]),
         ),
-        out_shape=[jax.ShapeDtypeStruct((1, rows, d), BF), jax.ShapeDtypeStruct(wide, BF)],
+        out_shape=[jax.ShapeDtypeStruct((1, rows, d), BF)]
+        + ([jax.ShapeDtypeStruct(wide, BF)] if begin else [jax.ShapeDtypeStruct(split, BF)] * 2),
         compiler_params=params(1),
         cost_estimate=cost(40, 20 << 20),
         name="attn_bwd",
-    )(lens, x, qkv, qkv, qkv, gmix, gmid, lse, inner, gathered, vec, *prev)
+    )(lens, core, x, qkv, qkv, qkv, gmix, gmid, lse, inner, gathered, vec, *prev)
 
 
 def place_blocks(table, pieces, blocks):
@@ -752,15 +784,6 @@
     return parts
 
 
-def sum_partner(grads):
-    dp = lax.axis_size("dp")
-    block = grads.reshape(dp // 2, 2, -1, grads.shape[1])
-    core = lax.axis_index("dp") % 2
-    mine = lax.dynamic_index_in_dim(block, core, 1, keepdims=False)
-    other = lax.dynamic_index_in_dim(block, 1 - core, 1, keepdims=False)
-    return mine, swap(other, "dp", 1)
-
-
 def sum_plane(mine, other):
     chip = lax.axis_index("dp") // 2
 
@@ -791,7 +814,9 @@
 def device_step(tokens, cotangent, lengths, perm, ln1_gain, ln1_bias, w_qkv, w_out,
                ln2_gain, ln2_bias, w_up, w_down):
     zs = lax.axis_size("fsdp")
-    devices = lax.axis_size("dp") * zs
+    dp = lax.axis_size("dp")
+    devices = dp * zs
+    core = (lax.axis_index("dp") % 2).reshape(1).astype(jnp.int32)
     z = lax.axis_index("fsdp")
     slots, rows, d = tokens.shape
     mb = slots // zs
@@ -824,31 +849,30 @@
         return exchange(parts, "fsdp")
 
     x = deal(tokens)
-    x, cotangent = lax.optimization_barrier((x, cotangent))
     cot = deal(cotangent)
     qkv, low, lse = attn_fwd(lens, x, gathered, vec)
     out, mid = mlp_fwd(lens, low, x, rest, wdown, vec)
     cot, out = lax.optimization_barrier((cot, out))
-    gmid, gmix, inner, gmain, gdown = mlp_bwd(lens, low, mid, cot, rest, wdown, vec, share)
+    gmid, gmix, inner, keep, give, gdown = mlp_bwd(lens, core, low, mid, cot, rest, wdown, vec, share, dp)
     if share % 8:
         gtop = gdown[:, :ff].reshape(d, chunks, d).transpose(1, 0, 2)
         gtop = gtop.reshape(devices, chunks, share, d).transpose(0, 2, 1, 3).reshape(d, ff)
         gdown = jnp.concatenate([gtop, gdown[:, ff:]], axis=1)
     early = lax.psum_scatter(gdown, ("dp", "fsdp"), scatter_dimension=0, tiled=True)
-    halves = sum_partner(gmain)
+    halves = (keep, swap(give, "dp", 1))
+    planes = sum_plane(*halves)
     outs = give_back(out)
     grads = []
     prev = ()
     for m in range(mb):
-        dx, gw = attn_bwd(m, prev, lens, x, qkv, gmix, gmid, lse, inner, gathered, vec)
-        prev = (gw,)
+        dx, *gw = attn_bwd(m, prev, dp, lens, core, x, qkv, gmix, gmid, lse, inner, gathered, vec)
+        prev = tuple(gw)
         grads += give_back(dx)
         if m == 0:
-            planes = sum_plane(*halves)
-    halves = sum_partner(gw)
+            main = sum_line(planes)
+    halves = (gw[0], swap(gw[1], "dp", 1))
     late = sum_plane(*halves)
     late = sum_line(late)
-    main = sum_line(planes)
     block_out = place_blocks(send_at, outs, slots)
     d_tokens = place_blocks(send_at.reshape(zs, mb).T.reshape(-1), grads, slots)
     early = early.astype(F32)

time: 709 us -> 735 us (1.037)
  waiting for transfers between devices: 215 us -> 241 us
    ppermute x43, waiting for transfers between devices: 215 us -> 241 us  [swap(): return lax.ppermute(x, axis, [(s, s ^ bits) for s in range(size)])]
    pallas_call x2, Pallas kernels: 66.5 us -> 53.9 us  [attn_bwd(): pl.pallas_call(functools.partial(attn_bwd_kernel, m=m, begin=begin), grid...]
    pallas_call x2, Pallas kernels: 15 us -> 26.3 us  [place_weights(): pl.pallas_call(kernel, grid_spec=pltpu.PrefetchScalarGridSpec(num_scalar_...]
  transfers between devices with their start and end apart: 44 -> 44, of which waited for: 14 -> 16; matrix products, arithmetic and copies ran while one was open for 8% -> 8% of each run, Pallas kernels for 16% -> 14%
where the time goes in v1:
time: 735 us; the launch traced here: 731 us
  waiting for transfers between devices  241 us (33%)
  Pallas kernels  208 us (28%)
  starting transfers between devices  199 us (27%)
  local copies, waits for them, and re-layouts  43.9 us (6%)
  other arithmetic  23.6 us (3%)
  between operations  14.6 us (2%)
    ppermute x43, waiting for transfers between devices, swap(): return lax.ppermute(x, axis, [(s, s ^ bits) for s in range(size)])  241 us
    ppermute x43, starting transfers between devices, swap(): return lax.ppermute(x, axis, [(s, s ^ bits) for s in range(size)])  199 us
    pallas_call x1, Pallas kernels, mlp_bwd(): pl.pallas_call(functools.partial(mlp_bwd_kernel, share=share), grid_spec=...  59.6 us
    pallas_call x2, Pallas kernels, attn_bwd(): pl.pallas_call(functools.partial(attn_bwd_kernel, m=m, begin=begin), grid...  53.9 us
    pallas_call x1, Pallas kernels, attn_fwd(): pl.pallas_call(attn_fwd_kernel, grid_spec=pltpu.PrefetchScalarGridSpec(nu...  29.6 us
    pallas_call x2, Pallas kernels, place_weights(): pl.pallas_call(kernel, grid_spec=pltpu.PrefetchScalarGridSpec(num_scalar_...  26.3 us
    pallas_call x1, Pallas kernels, mlp_fwd(): pl.pallas_call(mlp_fwd_kernel, grid_spec=pltpu.PrefetchScalarGridSpec(num...  24.8 us
    gather x8, local copies, waits for them, and re-layouts, deal(): jnp.take(array, send_at[b * mb:(b + 1) * mb], axis=0, mode='clip')  19.5 us
  transfers between devices with their start and end apart: 44, of which 16 were waited for; matrix products, arithmetic and copies ran while one was open for 8% of the time, Pallas kernels for 14%

profile of v1, /device:TPU:0, one launch (start us, length us, event | category | flops | bytes accessed | tf_op | source)
XLA Modules:
  0.0 730.6 jit_solution(17456356355297778163)
XLA Ops:
  9.8 4.1 collective-permute-start.7
  23.3 2.6 collective-permute-done.6
  27.9 5.3 collective-permute-start.9
  37.7 3.4 gather_fusion.2
  41.1 3.4 gather_fusion.3
  45.9 3.4 gather_fusion.4
  50.9 3.4 gather_fusion.1
  55.1 11.7 %collective-permute-done.15 = bf16[24,6912]{1,0:T(8,128)(2,1)S(1)} collective-permute-done((bf16[24,6912]{1,0:T(8,128)(2,1)S(1)}, bf16[24,6912]{1,0:T(8,128)(2,1)S(1)}, u32[]{:S(2)}, u32[]{:S(2)}) %collective-permute-start.15) | collective-permute-done | bytes 331808 | tf_op jit(solution)/shard_map/ppermute | solution.py:753
  70.3 2.7 collective-permute-start.1
  74.6 10.8 %collective-permute-done.3.refs_1_ = bf16[2,256,768]{2,1,0:T(8,128)(2,1)S(1)} collective-permute-done((bf16[2,256,768]{2,1,0:T(8,128)(2,1)}, bf16[2,256,768]{2,1,0:T(8,128)(2,1)S(1)}, u32[]{:S(2)}, u32[]{:S(2)}) %collective-permute-start.3) | collective-permute-done | bytes 786464 | tf_op jit(solution)/shard_map/ppermute | solution.py:753
  85.4 5.4 collective-permute-start.2
  90.8 31.2 %collective-permute-done.4.refs_2_ = bf16[2,256,768]{2,1,0:T(8,128)(2,1)S(1)} collective-permute-done((bf16[2,256,768]{2,1,0:T(8,128)(2,1)}, bf16[2,256,768]{2,1,0:T(8,128)(2,1)S(1)}, u32[]{:S(2)}, u32[]{:S(2)}) %collective-permute-start.4) | collective-permute-done | bytes 786464 | tf_op jit(solution)/shard_map/ppermute | solution.py:753
  125.5 4.6 collective-permute-done.refs_1_
  130.1 2.9 collective-permute-start.18
  133.0 2.8 pad_maximum_fusion.1
  135.9 52.8 %collective-permute-done.1.refs_2_ = bf16[2,256,768]{2,1,0:T(8,128)(2,1)S(1)} collective-permute-done((bf16[2,256,768]{2,1,0:T(8,128)(2,1)}, bf16[2,256,768]{2,1,0:T(8,128)(2,1)S(1)}, u32[]{:S(2)}, u32[]{:S(2)}) %collective-permute-start.1) | collective-permute-done | bytes 786464 | tf_op jit(solution)/shard_map/ppermute | solution.py:753
  190.1 3.4 place_blocks.5
  193.6 3.5 place_blocks.4
  197.1 5.3 pad_maximum_fusion
  202.6 4.8 place_weights.2.w_ref
  209.1 29.6 %attn_fwd.1 = (bf16[2,1024,2304]{2,1,0:T(8,128)(2,1)}, bf16[2,1024,768]{2,1,0:T(8,128)(2,1)}, f32[2,16,1024]{2,1,0:T(8,128)}) custom-call(s32[2]{0:T(128)} %fusion.22.lens, bf16[2,1024,768]{2,1,0:T(8,128)(2,1)} %bitcast.137, bf16[768,2432]{1,0:T(8,128)(2,1)} %place_weights.2.w_ref, f32[8,768]{1,0:T(8,128)} %pad_convert_fusion.vec_ref), custom_call_target="tpu_custom_call" | custom-call | flops 60000002048 | bytes 20971520 | tf_op jit(solution)/shard_map/attn_fwd/pallas_call | solution.py:127
  238.7 21.5 %place_weights.3 = (bf16[768,3840]{1,0:T(8,128)(2,1)}, bf16[3072,768]{1,0:T(8,128)(2,1)}) custom-call(s32[32]{0:T(128)} %pad_add_fusion.at, bf16[16,24,6912]{2,1,0:T(8,128)(2,1)} %bitcast.28.refs_0_, bf16[16,24,6912]{2,1,0:T(8,128)(2,1)} %collective-permute-done.19.refs_1_), custom_call_target="tpu_custom_call" | custom-call | flops 8000000000 | bytes 21233664 | tf_op jit(solution)/shard_map/place_weights/pallas_call | solution.py:732
  260.2 24.8 %mlp_fwd.1 = (bf16[2,1024,768]{2,1,0:T(8,128)(2,1)}, f32[2,1024,768]{2,1,0:T(8,128)}) custom-call(s32[2]{0:T(128)} %fusion.22.lens, bf16[2,1024,768]{2,1,0:T(8,128)(2,1)} %get-tuple-element.30.low_ref, bf16[2,1024,768]{2,1,0:T(8,128)(2,1)} %bitcast.138, f32[8,768]{1,0:T(8,128)} %pad_convert_fusion.vec_ref, bf16[768,3840]{1,0:T(8,128)(2,1)} %get-tuple-element.31.rest_ref, ...), custom_call_target="tpu_custom_call" | custom-call | flops 40000000000 | bytes 41943040 | tf_op jit(solution)/shard_map/mlp_fwd/pallas_call | solution.py:246
  285.0 59.6 %mlp_bwd.1 = (f32[2,1024,768]{2,1,0:T(8,128)}, bf16[2,1024,768]{2,1,0:T(8,128)(2,1)}, f32[2,16,1024]{2,1,0:T(8,128)}, bf16[4,96,3840]{2,1,0:T(8,128)(2,1)}, bf16...) custom-call(s32[2]{0:T(128)} %fusion.22.lens, s32[1]{0:T(128)} %bitcast.35.core, ...), custom_call_target="tpu_custom_call" | custom-call | flops 80000000000 | bytes 62914560 | tf_op jit(solution)/shard_map/mlp_bwd/pallas_call | solution.py:408
  345.1 39.1 %attn_bwd.2 = (bf16[1,1024,768]{2,1,0:T(8,128)(2,1)}, bf16[768,2432]{1,0:T(8,128)(2,1)}) custom-call(s32[2]{0:T(128)} %fusion.22.lens, s32[1]{0:T(128)} %bitcast.35.core, bf16[2,1024,768]{2,1,0:T(8,128)(2,1)} %bitcast.139, bf16[2,1024,2304]{2,1,0:T(8,128)(2,1)} %get-tuple-element.35.q_ref.k_ref.v_ref, ...), custom_call_target="tpu_custom_call" | custom-call | flops 40000000000 | bytes 20971520 | tf_op jit(solution)/shard_map/attn_bwd/pallas_call | solution.py:609
  384.1 14.8 %attn_bwd.3 = (bf16[1,1024,768]{2,1,0:T(8,128)(2,1)}, bf16[4,96,2432]{2,1,0:T(8,128)(2,1)}, bf16[4,96,2432]{2,1,0:T(8,128)(2,1)}) custom-call(s32[2]{0:T(128)} %fusion.22.lens, s32[1]{0:T(128)} %bitcast.35.core, bf16[2,1024,768]{2,1,0:T(8,128)(2,1)} %bitcast.140, bf16[2,1024,2304]{2,1,0:T(8,128)(2,1)} %get-tuple-element.35.q_ref.k_ref.v_ref, ...), custom_call_target="tpu_custom_call" | custom-call | flops 40000000000 | bytes 20971520 | tf_op jit(solution)/shard_map/attn_bwd/pallas_call | solution.py:609
  399.0 2.3 dynamic-slice_bitcast_fusion.4
  401.3 75.7 %collective-permute-start.26 = (bf16[1,256,768]{2,1,0:T(8,128)(2,1)S(1)}, bf16[1,256,768]{2,1,0:T(8,128)(2,1)S(1)}, u32[]{:S(2)}, u32[]{:S(2)}) collective-permute-start(bf16[1,256,768]{2,1,0:T(8,128)(2,1)S(1)} %get-tuple-element.66), channel_id=1, source_target_pairs={{0,1},{1,0},{2,3},{3,2},{4,5},{5,4},{6,7},{7,6},{8,9},{9,8},{10,11... | collective-permute-start | bytes 1179656 | tf_op jit(solution)/shard_map/ppermute | solution.py:753
  477.0 7.0 collective-permute-start.27
  488.0 21.3 %collective-permute-done.27.refs_6_ = bf16[1,256,768]{2,1,0:T(8,128)(2,1)S(1)} collective-permute-done((bf16[1,256,768]{2,1,0:T(8,128)(2,1)S(1)}, bf16[1,256,768]{2,1,0:T(8,128)(2,1)S(1)}, u32[]{:S(2)}, u32[]{:S(2)}) %collective-permute-start.27) | collective-permute-done | bytes 393248 | tf_op jit(solution)/shard_map/ppermute | solution.py:753
  509.3 2.9 collective-permute-done.28.refs_7_
  512.3 2.6 collective-permute-start.25
  518.4 22.6 %collective-permute-start.20 = (bf16[2,256,768]{2,1,0:T(8,128)(2,1)}, bf16[2,256,768]{2,1,0:T(8,128)(2,1)S(1)}, u32[]{:S(2)}, u32[]{:S(2)}) collective-permute-start(bf16[2,256,768]{2,1,0:T(8,128)(2,1)} %get-tuple-element.62), channel_id=1, source_target_pairs={{0,1},{1,0},{2,3},{3,2},{4,5},{5,4},{6,7},{7,6},{8,9},{9,8},{10,11... | collective-permute-start | bytes 2359304 | tf_op jit(solution)/shard_map/ppermute | solution.py:753
  541.0 3.6 collective-permute-done.24.refs_2_
  546.7 3.4 place_blocks.7
  550.1 16.2 %collective-permute-done.20.refs_1_ = bf16[2,256,768]{2,1,0:T(8,128)(2,1)S(1)} collective-permute-done((bf16[2,256,768]{2,1,0:T(8,128)(2,1)}, bf16[2,256,768]{2,1,0:T(8,128)(2,1)S(1)}, u32[]{:S(2)}, u32[]{:S(2)}) %collective-permute-start.20) | collective-permute-done | bytes 786464 | tf_op jit(solution)/shard_map/ppermute | solution.py:753
  566.3 50.4 %collective-permute-done.21.refs_2_ = bf16[2,256,768]{2,1,0:T(8,128)(2,1)S(1)} collective-permute-done((bf16[2,256,768]{2,1,0:T(8,128)(2,1)}, bf16[2,256,768]{2,1,0:T(8,128)(2,1)S(1)}, u32[]{:S(2)}, u32[]{:S(2)}) %collective-permute-start.21) | collective-permute-done | bytes 786464 | tf_op jit(solution)/shard_map/ppermute | solution.py:753
  617.9 3.4 place_blocks.6
  621.4 2.5 fusion.11
  623.9 10.0 %collective-permute-start.30 = (bf16[96,2432]{1,0:T(8,128)(2,1)S(1)}, bf16[96,2432]{1,0:T(8,128)(2,1)S(1)}, u32[]{:S(2)}, u32[]{:S(2)}) collective-permute-start(bf16[96,2432]{1,0:T(8,128)(2,1)S(1)} %get-tuple-element.57), channel_id=1, source_target_pairs={{0,8},{4,12},{8,0},{12,4},{16,24},{20,28},{24,16},{28,20},{1,9},{5... | collective-permute-start | bytes 1400840 | tf_op jit(solution)/shard_map/ppermute | solution.py:753
  639.4 5.9 collective-permute-done.30
  645.4 16.0 %collective-permute-done.31 = bf16[96,2432]{1,0:T(8,128)(2,1)S(1)} collective-permute-done((bf16[96,2432]{1,0:T(8,128)(2,1)S(1)}, bf16[96,2432]{1,0:T(8,128)(2,1)S(1)}, u32[]{:S(2)}, u32[]{:S(2)}) %collective-permute-start.31) | collective-permute-done | bytes 466976 | tf_op jit(solution)/shard_map/ppermute | solution.py:753
  662.9 14.4 %collective-permute-start.33 = (bf16[24,2432]{1,0:T(8,128)(2,1)S(1)}, bf16[24,2432]{1,0:T(8,128)(2,1)S(1)}, u32[]{:S(2)}, u32[]{:S(2)}) collective-permute-start(bf16[24,2432]{1,0:T(8,128)(2,1)S(1)} %get-tuple-element.77), channel_id=1, source_target_pairs={{0,1},{1,0},{2,3},{3,2},{4,5},{5,4},{6,7},{7,6},{8,9},{9,8},{10,11... | collective-permute-start | bytes 350216 | tf_op jit(solution)/shard_map/ppermute | solution.py:753
  677.3 6.1 collective-permute-start.34
  686.5 16.1 %collective-permute-start.40 = (bf16[24,3840]{1,0:T(8,128)(2,1)S(1)}, bf16[24,3840]{1,0:T(8,128)(2,1)S(1)}, u32[]{:S(2)}, u32[]{:S(2)}) collective-permute-start(bf16[24,3840]{1,0:T(8,128)(2,1)S(1)} %get-tuple-element.74), channel_id=1, source_target_pairs={{0,1},{1,0},{2,3},{3,2},{4,5},{5,4},{6,7},{7,6},{8,9},{9,8},{10,11... | collective-permute-start | bytes 552968 | tf_op jit(solution)/shard_map/ppermute | solution.py:753
  702.6 2.4 collective-permute-start.42
  706.5 3.4 collective-permute-done.40
  709.9 6.1 collective-permute-done.41
  (161 shorter events, 64.7 us)
Async XLA Ops:
  7.2 710.3 %reduce-scatter.4.cloned.1.call-start = ((), (), s32[]{:S(2)}) async-start(), calls=%async_computation.1 | async-start | bytes 5068800
  9.8 13.5 %collective-permute-start.7 = (bf16[24,2432]{1,0:T(8,128)(2,1)}, bf16[24,2432]{1,0:T(8,128)(2,1)}, u32[]{:S(2)}, u32[]{:S(2)}) collective-permute-start(bf16[24,2432]{1,0:T(8,128)(2,1)} %get-tuple-element.83), channel_id=1, source_target_pairs={{0,2},{1,3},{2,0},{3,1},{4,6},{5,7},{6,4},{7,5},{8,10},{9,11},{10,... | collective-permute-start | bytes 350216 | tf_op jit(solution)/shard_map/ppermute | solution.py:753
  13.9 9.4 %collective-permute-start.8 = (bf16[24,2432]{1,0:T(8,128)(2,1)}, bf16[24,2432]{1,0:T(8,128)(2,1)}, u32[]{:S(2)}, u32[]{:S(2)}) collective-permute-start(bf16[24,2432]{1,0:T(8,128)(2,1)} %get-tuple-element.83), channel_id=1, source_target_pairs={{0,3},{1,2},{2,1},{3,0},{4,7},{5,6},{6,5},{7,4},{8,11},{9,10},{10,... | collective-permute-start | bytes 350216 | tf_op jit(solution)/shard_map/ppermute | solution.py:753
  15.2 10.6 %collective-permute-start.6 = (bf16[24,2432]{1,0:T(8,128)(2,1)}, bf16[24,2432]{1,0:T(8,128)(2,1)}, u32[]{:S(2)}, u32[]{:S(2)}) collective-permute-start(bf16[24,2432]{1,0:T(8,128)(2,1)} %get-tuple-element.83), channel_id=1, source_target_pairs={{0,1},{1,0},{2,3},{3,2},{4,5},{5,4},{6,7},{7,6},{8,9},{9,8},{10,11... | collective-permute-start | bytes 350216 | tf_op jit(solution)/shard_map/ppermute | solution.py:753
  18.1 36.1 %collective-permute-start.13 = (bf16[24,6912]{1,0:T(8,128)(2,1)S(1)}, bf16[24,6912]{1,0:T(8,128)(2,1)}, u32[]{:S(2)}, u32[]{:S(2)}) collective-permute-start(bf16[24,6912]{1,0:T(8,128)(2,1)S(1)} %constant_dynamic-update-slice_fusion), channel_id=1, source_target_pairs={{0,1},{1,0},{2,3},{3,2},{4,5},{5,4},{6,7},{7,6},{8,9},{9,8},{10,11... | collective-permute-start | bytes 995336 | tf_op jit(solution)/shard_map/ppermute | solution.py:753
  20.0 35.0 %collective-permute-start.14 = (bf16[24,6912]{1,0:T(8,128)(2,1)S(1)}, bf16[24,6912]{1,0:T(8,128)(2,1)}, u32[]{:S(2)}, u32[]{:S(2)}) collective-permute-start(bf16[24,6912]{1,0:T(8,128)(2,1)S(1)} %constant_dynamic-update-slice_fusion), channel_id=1, source_target_pairs={{0,2},{1,3},{2,0},{3,1},{4,6},{5,7},{6,4},{7,5},{8,10},{9,11},{10,... | collective-permute-start | bytes 995336 | tf_op jit(solution)/shard_map/ppermute | solution.py:753
  27.9 40.6 %collective-permute-start.9 = (bf16[4,24,2432]{2,1,0:T(8,128)(2,1)}, bf16[4,24,2432]{2,1,0:T(8,128)(2,1)}, u32[]{:S(2)}, u32[]{:S(2)}) collective-permute-start(bf16[4,24,2432]{2,1,0:T(8,128)(2,1)} %get-tuple-element.81), channel_id=1, source_target_pairs={{0,8},{4,12},{8,0},{12,4},{16,24},{20,28},{24,16},{28,20},{1,9},{5... | collective-permute-start | bytes 1400840 | tf_op jit(solution)/shard_map/ppermute | solution.py:753
  33.2 35.8 %collective-permute-start.10 = (bf16[4,24,2432]{2,1,0:T(8,128)(2,1)}, bf16[4,24,2432]{2,1,0:T(8,128)(2,1)}, u32[]{:S(2)}, u32[]{:S(2)}) collective-permute-start(bf16[4,24,2432]{2,1,0:T(8,128)(2,1)} %get-tuple-element.81), channel_id=1, source_target_pairs={{0,16},{4,20},{8,24},{12,28},{16,0},{20,4},{24,8},{28,12},{1,17},{... | collective-permute-start | bytes 1400840 | tf_op jit(solution)/shard_map/ppermute | solution.py:753
  34.7 35.5 %collective-permute-start.11 = (bf16[4,24,2432]{2,1,0:T(8,128)(2,1)}, bf16[4,24,2432]{2,1,0:T(8,128)(2,1)}, u32[]{:S(2)}, u32[]{:S(2)}) collective-permute-start(bf16[4,24,2432]{2,1,0:T(8,128)(2,1)} %get-tuple-element.81), channel_id=1, source_target_pairs={{0,24},{4,28},{8,16},{12,20},{16,8},{20,12},{24,0},{28,4},{1,25},{... | collective-permute-start | bytes 1400840 | tf_op jit(solution)/shard_map/ppermute | solution.py:753
  54.2 12.5 %collective-permute-start.15 = (bf16[24,6912]{1,0:T(8,128)(2,1)S(1)}, bf16[24,6912]{1,0:T(8,128)(2,1)S(1)}, u32[]{:S(2)}, u32[]{:S(2)}) collective-permute-start(bf16[24,6912]{1,0:T(8,128)(2,1)S(1)} %constant_dynamic-update-slice_fusion), channel_id=1, source_target_pairs={{0,3},{1,2},{2,1},{3,0},{4,7},{5,6},{6,5},{7,4},{8,11},{9,10},{10,... | collective-permute-start | bytes 995336 | tf_op jit(solution)/shard_map/ppermute | solution.py:753
  55.0 30.4 %collective-permute-start.3 = (bf16[2,256,768]{2,1,0:T(8,128)(2,1)}, bf16[2,256,768]{2,1,0:T(8,128)(2,1)S(1)}, u32[]{:S(2)}, u32[]{:S(2)}) collective-permute-start(bf16[2,256,768]{2,1,0:T(8,128)(2,1)} %gather_fusion.6), channel_id=1, source_target_pairs={{0,1},{1,0},{2,3},{3,2},{4,5},{5,4},{6,7},{7,6},{8,9},{9,8},{10,11... | collective-permute-start | bytes 2359304 | tf_op jit(solution)/shard_map/ppermute | solution.py:753
  66.8 55.2 %collective-permute-start.4 = (bf16[2,256,768]{2,1,0:T(8,128)(2,1)}, bf16[2,256,768]{2,1,0:T(8,128)(2,1)S(1)}, u32[]{:S(2)}, u32[]{:S(2)}) collective-permute-start(bf16[2,256,768]{2,1,0:T(8,128)(2,1)} %gather_fusion.7), channel_id=1, source_target_pairs={{0,2},{1,3},{2,0},{3,1},{4,6},{5,7},{6,4},{7,5},{8,10},{9,11},{10,... | collective-permute-start | bytes 2359304 | tf_op jit(solution)/shard_map/ppermute | solution.py:753
  68.6 55.4 %collective-permute-start.5 = (bf16[2,256,768]{2,1,0:T(8,128)(2,1)}, bf16[2,256,768]{2,1,0:T(8,128)(2,1)S(1)}, u32[]{:S(2)}, u32[]{:S(2)}) collective-permute-start(bf16[2,256,768]{2,1,0:T(8,128)(2,1)} %gather_fusion.8), channel_id=1, source_target_pairs={{0,3},{1,2},{2,1},{3,0},{4,7},{5,6},{6,5},{7,4},{8,11},{9,10},{10,... | collective-permute-start | bytes 2359304 | tf_op jit(solution)/shard_map/ppermute | solution.py:753
  69.0 61.1 %collective-permute-start = (bf16[2,256,768]{2,1,0:T(8,128)(2,1)}, bf16[2,256,768]{2,1,0:T(8,128)(2,1)S(1)}, u32[]{:S(2)}, u32[]{:S(2)}) collective-permute-start(bf16[2,256,768]{2,1,0:T(8,128)(2,1)} %gather_fusion.2), channel_id=1, source_target_pairs={{0,1},{1,0},{2,3},{3,2},{4,5},{5,4},{6,7},{7,6},{8,9},{9,8},{10,11... | collective-permute-start | bytes 2359304 | tf_op jit(solution)/shard_map/ppermute | solution.py:753
  70.3 118.4 %collective-permute-start.1 = (bf16[2,256,768]{2,1,0:T(8,128)(2,1)}, bf16[2,256,768]{2,1,0:T(8,128)(2,1)S(1)}, u32[]{:S(2)}, u32[]{:S(2)}) collective-permute-start(bf16[2,256,768]{2,1,0:T(8,128)(2,1)} %gather_fusion.3), channel_id=1, source_target_pairs={{0,2},{1,3},{2,0},{3,1},{4,6},{5,7},{6,4},{7,5},{8,10},{9,11},{10,... | collective-permute-start | bytes 2359304 | tf_op jit(solution)/shard_map/ppermute | solution.py:753
  73.0 60.1 %copy-start.4 = (bf16[1,4,24,2432]{3,2,1,0:T(8,128)(2,1)S(1)}, bf16[1,4,24,2432]{3,2,1,0:T(8,128)(2,1)}, u32[]{:S(2)}) copy-start(bf16[1,4,24,2432]{3,2,1,0:T(8,128)(2,1)} %get-tuple-element.80) | copy-start | bytes 1400836
  85.4 108.2 %collective-permute-start.2 = (bf16[2,256,768]{2,1,0:T(8,128)(2,1)S(1)}, bf16[2,256,768]{2,1,0:T(8,128)(2,1)}, u32[]{:S(2)}, u32[]{:S(2)}) collective-permute-start(bf16[2,256,768]{2,1,0:T(8,128)(2,1)S(1)} %copy-done.7), channel_id=1, source_target_pairs={{0,3},{1,2},{2,1},{3,0},{4,7},{5,6},{6,5},{7,4},{8,11},{9,10},{10,... | collective-permute-start | bytes 2359304 | tf_op jit(solution)/shard_map/ppermute | solution.py:753
  122.0 75.1 %collective-permute-start.16 = (bf16[4,24,6912]{2,1,0:T(8,128)(2,1)S(1)}, bf16[4,24,6912]{2,1,0:T(8,128)(2,1)}, u32[]{:S(2)}, u32[]{:S(2)}) collective-permute-start(bf16[4,24,6912]{2,1,0:T(8,128)(2,1)S(1)} %get-tuple-element.73), channel_id=1, source_target_pairs={{0,8},{4,12},{8,0},{12,4},{16,24},{20,28},{24,16},{28,20},{1,9},{5... | collective-permute-start | bytes 3981320 | tf_op jit(solution)/shard_map/ppermute | solution.py:753
  124.0 65.4 %copy-start.18 = (bf16[2,256,768]{2,1,0:T(8,128)(2,1)}, bf16[2,256,768]{2,1,0:T(8,128)(2,1)S(1)}, u32[]{:S(2)}) copy-start(bf16[2,256,768]{2,1,0:T(8,128)(2,1)S(1)} %collective-permute-done.5.refs_3_) | copy-start | bytes 2359300
  124.0 73.1 %collective-permute-start.17 = (bf16[4,24,6912]{2,1,0:T(8,128)(2,1)S(1)}, bf16[4,24,6912]{2,1,0:T(8,128)(2,1)}, u32[]{:S(2)}, u32[]{:S(2)}) collective-permute-start(bf16[4,24,6912]{2,1,0:T(8,128)(2,1)S(1)} %get-tuple-element.73), channel_id=1, source_target_pairs={{0,16},{4,20},{8,24},{12,28},{16,0},{20,4},{24,8},{28,12},{1,17},{... | collective-permute-start | bytes 3981320 | tf_op jit(solution)/shard_map/ppermute | solution.py:753
  130.1 67.0 %collective-permute-start.18 = (bf16[4,24,6912]{2,1,0:T(8,128)(2,1)S(1)}, bf16[4,24,6912]{2,1,0:T(8,128)(2,1)}, u32[]{:S(2)}, u32[]{:S(2)}) collective-permute-start(bf16[4,24,6912]{2,1,0:T(8,128)(2,1)S(1)} %get-tuple-element.73), channel_id=1, source_target_pairs={{0,24},{4,28},{8,16},{12,20},{16,8},{20,12},{24,0},{28,4},{1,25},{... | collective-permute-start | bytes 3981320 | tf_op jit(solution)/shard_map/ppermute | solution.py:753
  133.0 56.5 %copy-start.23 = (s32[1,8]{1,0:T(1,128)S(1)}, s32[1,8]{1,0:T(1,128)}, u32[]{:S(2)}) copy-start(s32[1,8]{1,0:T(1,128)} %param.14) | copy-start | bytes 100
  188.6 14.0 %collective-permute-start.12 = (bf16[16,24,2432]{2,1,0:T(8,128)(2,1)}, bf16[16,24,2432]{2,1,0:T(8,128)(2,1)}, u32[]{:S(2)}, u32[]{:S(2)}) collective-permute-start(bf16[16,24,2432]{2,1,0:T(8,128)(2,1)} %bitcast.16.refs_0_), channel_id=1, source_target_pairs={{0,4},{4,0},{8,12},{12,8},{16,20},{20,16},{24,28},{28,24},{1,5},{5... | collective-permute-start | bytes 5603336 | tf_op jit(solution)/shard_map/ppermute | solution.py:753
  202.4 36.3 %collective-permute-start.19 = (bf16[16,24,6912]{2,1,0:T(8,128)(2,1)}, bf16[16,24,6912]{2,1,0:T(8,128)(2,1)}, u32[]{:S(2)}, u32[]{:S(2)}) collective-permute-start(bf16[16,24,6912]{2,1,0:T(8,128)(2,1)} %bitcast.28.refs_0_), channel_id=1, source_target_pairs={{0,4},{4,0},{8,12},{12,8},{16,20},{20,16},{24,28},{28,24},{1,5},{5... | collective-permute-start | bytes 15925256 | tf_op jit(solution)/shard_map/ppermute | solution.py:753
  344.7 290.7 %collective-permute-start.36 = (bf16[4,96,3840]{2,1,0:T(8,128)(2,1)}, bf16[4,96,3840]{2,1,0:T(8,128)(2,1)}, u32[]{:S(2)}, u32[]{:S(2)}) collective-permute-start(bf16[4,96,3840]{2,1,0:T(8,128)(2,1)} %get-tuple-element.48), channel_id=1, source_target_pairs={{0,4},{4,0},{8,12},{12,8},{16,20},{20,16},{24,28},{28,24},{1,5},{5... | collective-permute-start | bytes 8847368 | tf_op jit(solution)/shard_map/ppermute | solution.py:753
  399.0 86.5 %copy-start.5 = (bf16[1,1024,768]{2,1,0:T(8,128)(2,1)S(1)}, bf16[1,1024,768]{2,1,0:T(8,128)(2,1)}, u32[]{:S(2)}) copy-start(bf16[1,1024,768]{2,1,0:T(8,128)(2,1)} %get-tuple-element.42) | copy-start | bytes 4718596
  401.3 86.7 %collective-permute-start.26 = (bf16[1,256,768]{2,1,0:T(8,128)(2,1)S(1)}, bf16[1,256,768]{2,1,0:T(8,128)(2,1)S(1)}, u32[]{:S(2)}, u32[]{:S(2)}) collective-permute-start(bf16[1,256,768]{2,1,0:T(8,128)(2,1)S(1)} %get-tuple-element.66), channel_id=1, source_target_pairs={{0,1},{1,0},{2,3},{3,2},{4,5},{5,4},{6,7},{7,6},{8,9},{9,8},{10,11... | collective-permute-start | bytes 1179656 | tf_op jit(solution)/shard_map/ppermute | solution.py:753
  477.0 32.3 %collective-permute-start.27 = (bf16[1,256,768]{2,1,0:T(8,128)(2,1)S(1)}, bf16[1,256,768]{2,1,0:T(8,128)(2,1)S(1)}, u32[]{:S(2)}, u32[]{:S(2)}) collective-permute-start(bf16[1,256,768]{2,1,0:T(8,128)(2,1)S(1)} %get-tuple-element.65), channel_id=1, source_target_pairs={{0,2},{1,3},{2,0},{3,1},{4,6},{5,7},{6,4},{7,5},{8,10},{9,11},{10,... | collective-permute-start | bytes 1179656 | tf_op jit(solution)/shard_map/ppermute | solution.py:753
  484.0 28.3 %collective-permute-start.28 = (bf16[1,256,768]{2,1,0:T(8,128)(2,1)S(1)}, bf16[1,256,768]{2,1,0:T(8,128)(2,1)S(1)}, u32[]{:S(2)}, u32[]{:S(2)}) collective-permute-start(bf16[1,256,768]{2,1,0:T(8,128)(2,1)S(1)} %get-tuple-element.64), channel_id=1, source_target_pairs={{0,3},{1,2},{2,1},{3,0},{4,7},{5,6},{6,5},{7,4},{8,11},{9,10},{10,... | collective-permute-start | bytes 1179656 | tf_op jit(solution)/shard_map/ppermute | solution.py:753
  485.4 135.9 %collective-permute-start.29 = (bf16[4,96,2432]{2,1,0:T(8,128)(2,1)}, bf16[4,96,2432]{2,1,0:T(8,128)(2,1)}, u32[]{:S(2)}, u32[]{:S(2)}) collective-permute-start(bf16[4,96,2432]{2,1,0:T(8,128)(2,1)} %get-tuple-element.46), channel_id=1, source_target_pairs={{0,4},{4,0},{8,12},{12,8},{16,20},{20,16},{24,28},{28,24},{1,5},{5... | collective-permute-start | bytes 5603336 | tf_op jit(solution)/shard_map/ppermute | solution.py:753
  488.0 30.4 %collective-permute-start.23 = (bf16[1,256,768]{2,1,0:T(8,128)(2,1)}, bf16[1,256,768]{2,1,0:T(8,128)(2,1)}, u32[]{:S(2)}, u32[]{:S(2)}) collective-permute-start(bf16[1,256,768]{2,1,0:T(8,128)(2,1)} %get-tuple-element.70), channel_id=1, source_target_pairs={{0,1},{1,0},{2,3},{3,2},{4,5},{5,4},{6,7},{7,6},{8,9},{9,8},{10,11... | collective-permute-start | bytes 1179656 | tf_op jit(solution)/shard_map/ppermute | solution.py:753
  509.3 35.3 %collective-permute-start.24 = (bf16[1,256,768]{2,1,0:T(8,128)(2,1)}, bf16[1,256,768]{2,1,0:T(8,128)(2,1)}, u32[]{:S(2)}, u32[]{:S(2)}) collective-permute-start(bf16[1,256,768]{2,1,0:T(8,128)(2,1)} %get-tuple-element.69), channel_id=1, source_target_pairs={{0,2},{1,3},{2,0},{3,1},{4,6},{5,7},{6,4},{7,5},{8,10},{9,11},{10,... | collective-permute-start | bytes 1179656 | tf_op jit(solution)/shard_map/ppermute | solution.py:753
  512.3 32.4 %collective-permute-start.25 = (bf16[1,256,768]{2,1,0:T(8,128)(2,1)S(1)}, bf16[1,256,768]{2,1,0:T(8,128)(2,1)}, u32[]{:S(2)}, u32[]{:S(2)}) collective-permute-start(bf16[1,256,768]{2,1,0:T(8,128)(2,1)S(1)} %get-tuple-element.68), channel_id=1, source_target_pairs={{0,3},{1,2},{2,1},{3,0},{4,7},{5,6},{6,5},{7,4},{8,11},{9,10},{10,... | collective-permute-start | bytes 1179656 | tf_op jit(solution)/shard_map/ppermute | solution.py:753
  518.4 47.9 %collective-permute-start.20 = (bf16[2,256,768]{2,1,0:T(8,128)(2,1)}, bf16[2,256,768]{2,1,0:T(8,128)(2,1)S(1)}, u32[]{:S(2)}, u32[]{:S(2)}) collective-permute-start(bf16[2,256,768]{2,1,0:T(8,128)(2,1)} %get-tuple-element.62), channel_id=1, source_target_pairs={{0,1},{1,0},{2,3},{3,2},{4,5},{5,4},{6,7},{7,6},{8,9},{9,8},{10,11... | collective-permute-start | bytes 2359304 | tf_op jit(solution)/shard_map/ppermute | solution.py:753
  544.6 72.1 %collective-permute-start.21 = (bf16[2,256,768]{2,1,0:T(8,128)(2,1)}, bf16[2,256,768]{2,1,0:T(8,128)(2,1)S(1)}, u32[]{:S(2)}, u32[]{:S(2)}) collective-permute-start(bf16[2,256,768]{2,1,0:T(8,128)(2,1)} %get-tuple-element.61), channel_id=1, source_target_pairs={{0,2},{1,3},{2,0},{3,1},{4,6},{5,7},{6,4},{7,5},{8,10},{9,11},{10,... | collective-permute-start | bytes 2359304 | tf_op jit(solution)/shard_map/ppermute | solution.py:753
  544.6 72.1 %collective-permute-start.22 = (bf16[2,256,768]{2,1,0:T(8,128)(2,1)}, bf16[2,256,768]{2,1,0:T(8,128)(2,1)S(1)}, u32[]{:S(2)}, u32[]{:S(2)}) collective-permute-start(bf16[2,256,768]{2,1,0:T(8,128)(2,1)} %get-tuple-element.60), channel_id=1, source_target_pairs={{0,3},{1,2},{2,1},{3,0},{4,7},{5,6},{6,5},{7,4},{8,11},{9,10},{10,... | collective-permute-start | bytes 2359304 | tf_op jit(solution)/shard_map/ppermute | solution.py:753
  623.9 21.5 %collective-permute-start.30 = (bf16[96,2432]{1,0:T(8,128)(2,1)S(1)}, bf16[96,2432]{1,0:T(8,128)(2,1)S(1)}, u32[]{:S(2)}, u32[]{:S(2)}) collective-permute-start(bf16[96,2432]{1,0:T(8,128)(2,1)S(1)} %get-tuple-element.57), channel_id=1, source_target_pairs={{0,8},{4,12},{8,0},{12,4},{16,24},{20,28},{24,16},{28,20},{1,9},{5... | collective-permute-start | bytes 1400840 | tf_op jit(solution)/shard_map/ppermute | solution.py:753
  633.8 27.6 %collective-permute-start.31 = (bf16[96,2432]{1,0:T(8,128)(2,1)S(1)}, bf16[96,2432]{1,0:T(8,128)(2,1)S(1)}, u32[]{:S(2)}, u32[]{:S(2)}) collective-permute-start(bf16[96,2432]{1,0:T(8,128)(2,1)S(1)} %get-tuple-element.59), channel_id=1, source_target_pairs={{0,16},{4,20},{8,24},{12,28},{16,0},{20,4},{24,8},{28,12},{1,17},{... | collective-permute-start | bytes 1400840 | tf_op jit(solution)/shard_map/ppermute | solution.py:753
  633.8 27.6 %collective-permute-start.32 = (bf16[96,2432]{1,0:T(8,128)(2,1)S(1)}, bf16[96,2432]{1,0:T(8,128)(2,1)S(1)}, u32[]{:S(2)}, u32[]{:S(2)}) collective-permute-start(bf16[96,2432]{1,0:T(8,128)(2,1)S(1)} %get-tuple-element.58), channel_id=1, source_target_pairs={{0,24},{4,28},{8,16},{12,20},{16,8},{20,12},{24,0},{28,4},{1,25},{... | collective-permute-start | bytes 1400840 | tf_op jit(solution)/shard_map/ppermute | solution.py:753
  637.4 46.0 %collective-permute-start.37 = (bf16[96,3840]{1,0:T(8,128)(2,1)S(1)}, bf16[96,3840]{1,0:T(8,128)(2,1)S(1)}, u32[]{:S(2)}, u32[]{:S(2)}) collective-permute-start(bf16[96,3840]{1,0:T(8,128)(2,1)S(1)} %get-tuple-element.54), channel_id=1, source_target_pairs={{0,8},{4,12},{8,0},{12,4},{16,24},{20,28},{24,16},{28,20},{1,9},{5... | collective-permute-start | bytes 2211848 | tf_op jit(solution)/shard_map/ppermute | solution.py:753
  639.4 45.4 %collective-permute-start.38 = (bf16[96,3840]{1,0:T(8,128)(2,1)S(1)}, bf16[96,3840]{1,0:T(8,128)(2,1)S(1)}, u32[]{:S(2)}, u32[]{:S(2)}) collective-permute-start(bf16[96,3840]{1,0:T(8,128)(2,1)S(1)} %get-tuple-element.56), channel_id=1, source_target_pairs={{0,16},{4,20},{8,24},{12,28},{16,0},{20,4},{24,8},{28,12},{1,17},{... | collective-permute-start | bytes 2211848 | tf_op jit(solution)/shard_map/ppermute | solution.py:753
  645.4 39.5 %collective-permute-start.39 = (bf16[96,3840]{1,0:T(8,128)(2,1)S(1)}, bf16[96,3840]{1,0:T(8,128)(2,1)S(1)}, u32[]{:S(2)}, u32[]{:S(2)}) collective-permute-start(bf16[96,3840]{1,0:T(8,128)(2,1)S(1)} %get-tuple-element.55), channel_id=1, source_target_pairs={{0,24},{4,28},{8,16},{12,20},{16,8},{20,12},{24,0},{28,4},{1,25},{... | collective-permute-start | bytes 2211848 | tf_op jit(solution)/shard_map/ppermute | solution.py:753
  662.9 39.7 %collective-permute-start.33 = (bf16[24,2432]{1,0:T(8,128)(2,1)S(1)}, bf16[24,2432]{1,0:T(8,128)(2,1)S(1)}, u32[]{:S(2)}, u32[]{:S(2)}) collective-permute-start(bf16[24,2432]{1,0:T(8,128)(2,1)S(1)} %get-tuple-element.77), channel_id=1, source_target_pairs={{0,1},{1,0},{2,3},{3,2},{4,5},{5,4},{6,7},{7,6},{8,9},{9,8},{10,11... | collective-permute-start | bytes 350216 | tf_op jit(solution)/shard_map/ppermute | solution.py:753
  677.3 27.7 %collective-permute-start.34 = (bf16[24,2432]{1,0:T(8,128)(2,1)S(1)}, bf16[24,2432]{1,0:T(8,128)(2,1)S(1)}, u32[]{:S(2)}, u32[]{:S(2)}) collective-permute-start(bf16[24,2432]{1,0:T(8,128)(2,1)S(1)} %get-tuple-element.79), channel_id=1, source_target_pairs={{0,2},{1,3},{2,0},{3,1},{4,6},{5,7},{6,4},{7,5},{8,10},{9,11},{10,... | collective-permute-start | bytes 350216 | tf_op jit(solution)/shard_map/ppermute | solution.py:753
  683.4 21.6 %collective-permute-start.35 = (bf16[24,2432]{1,0:T(8,128)(2,1)S(1)}, bf16[24,2432]{1,0:T(8,128)(2,1)S(1)}, u32[]{:S(2)}, u32[]{:S(2)}) collective-permute-start(bf16[24,2432]{1,0:T(8,128)(2,1)S(1)} %get-tuple-element.78), channel_id=1, source_target_pairs={{0,3},{1,2},{2,1},{3,0},{4,7},{5,6},{6,5},{7,4},{8,11},{9,10},{10,... | collective-permute-start | bytes 350216 | tf_op jit(solution)/shard_map/ppermute | solution.py:753
  686.5 23.5 %collective-permute-start.40 = (bf16[24,3840]{1,0:T(8,128)(2,1)S(1)}, bf16[24,3840]{1,0:T(8,128)(2,1)S(1)}, u32[]{:S(2)}, u32[]{:S(2)}) collective-permute-start(bf16[24,3840]{1,0:T(8,128)(2,1)S(1)} %get-tuple-element.74), channel_id=1, source_target_pairs={{0,1},{1,0},{2,3},{3,2},{4,5},{5,4},{6,7},{7,6},{8,9},{9,8},{10,11... | collective-permute-start | bytes 552968 | tf_op jit(solution)/shard_map/ppermute | solution.py:753
  702.6 13.5 %collective-permute-start.41 = (bf16[24,3840]{1,0:T(8,128)(2,1)S(1)}, bf16[24,3840]{1,0:T(8,128)(2,1)S(1)}, u32[]{:S(2)}, u32[]{:S(2)}) collective-permute-start(bf16[24,3840]{1,0:T(8,128)(2,1)S(1)} %get-tuple-element.76), channel_id=1, source_target_pairs={{0,2},{1,3},{2,0},{3,1},{4,6},{5,7},{6,4},{7,5},{8,10},{9,11},{10,... | collective-permute-start | bytes 552968 | tf_op jit(solution)/shard_map/ppermute | solution.py:753
  702.6 13.4 %collective-permute-start.42 = (bf16[24,3840]{1,0:T(8,128)(2,1)S(1)}, bf16[24,3840]{1,0:T(8,128)(2,1)S(1)}, u32[]{:S(2)}, u32[]{:S(2)}) collective-permute-start(bf16[24,3840]{1,0:T(8,128)(2,1)S(1)} %get-tuple-element.75), channel_id=1, source_target_pairs={{0,3},{1,2},{2,1},{3,0},{4,7},{5,6},{6,5},{7,4},{8,11},{9,10},{10,... | collective-permute-start | bytes 552968 | tf_op jit(solution)/shard_map/ppermute | solution.py:753
  (20 other events, 314.8 us)
Sparse Core Ops, SparseCore 0:
  515.0 149.3 reduce-scatter.3

commit v2 on v1

--- a/solution.py
+++ b/solution.py
@@ -280,7 +280,7 @@
 def mlp_bwd_kernel(lens, core, low_ref, mid_ref, cot_ref, vec_ref, rest_ref, wd_ref,
                    gmid_ref, gmix_ref, inner_ref, keep_ref, give_ref, gdown_ref,
                    wout_ref, wup_ref, wdown_ref, aout_ref, aup_ref, adown_ref, gvec_ref, e2_ref,
-                   stage_ref, down_ref, sem, half_sem, *, share):
+                   stage_ref, down_ref, sem, half_sem, down_sem, *, share):
     m = pl.program_id(0)
     i = pl.program_id(1)
     d = mid_ref.shape[2]
@@ -358,14 +358,13 @@
 
     @pl.when(final)
     def _():
-        main = d + ff
-        stage_ref[:, 0:d] = aout_ref[...].astype(BF)
-        stage_ref[:, d:main] = aup_ref[...].astype(BF)
         each = keep_ref.shape[1]
 
-        def halves(step):
+        def halves(step, ready):
             for n in range(2 * keep_ref.shape[0]):
-                src = stage_ref.at[n * each:(n + 1) * each, :]
+                at = slice(n * each, (n + 1) * each)
+                ready(at)
+                src = stage_ref.at[at, :]
 
                 @pl.when(core[0] == n % 2)
                 def _():
@@ -375,27 +374,43 @@
                 def _():
                     step(pltpu.make_async_copy(src, give_ref.at[n // 2], half_sem.at[n]))
 
-        halves(lambda c: c.start())
+        def lower(at):
+            stage_ref[at, 0:d] = aout_ref[at, :].astype(BF)
+            stage_ref[at, d:] = aup_ref[at, :].astype(BF)
+
+        halves(lambda c: c.start(), lower)
+        down_ref[:, ff:ff + 128] = jnp.transpose(gvec_ref[...]).astype(BF)
         if share % 8 == 0:
+            pair = 2 * share
+
+            def leave(e):
+                at = pl.ds(pl.multiple_of(pair * e, 16), pair)
+                return pltpu.make_async_copy(down_ref.at[at, :], gdown_ref.at[at, :], down_sem.at[e])
 
             def regroup(e, carry):
                 for c in range(chunks):
-                    at = 2 * chunks * share * e + c * share
+                    at = chunks * pair * e + c * share
                     one = adown_ref[pl.ds(pl.multiple_of(at, 8), share), :]
                     two = adown_ref[pl.ds(pl.multiple_of(at + chunks * share, 8), share), :]
                     both = jnp.concatenate([one, two], axis=0).astype(BF)
-                    down_ref[pl.ds(pl.multiple_of(2 * share * e, 16), 2 * share), c * d:(c + 1) * d] = both
+                    down_ref[pl.ds(pl.multiple_of(pair * e, 16), pair), c * d:(c + 1) * d] = both
+                leave(e).start()
                 return carry
 
-            lax.fori_loop(0, d // (2 * share), regroup, 0)
+            def settle(e, carry):
+                leave(e).wait()
+                return carry
+
+            lax.fori_loop(0, d // pair, regroup, 0)
+            halves(lambda c: c.wait(), lambda at: None)
+            lax.fori_loop(0, d // pair, settle, 0)
         else:
             for c in range(chunks):
                 down_ref[:, c * d:(c + 1) * d] = adown_ref[c * d:(c + 1) * d, :].astype(BF)
-        down_ref[:, ff:ff + 128] = jnp.transpose(gvec_ref[...]).astype(BF)
-        last = pltpu.make_async_copy(down_ref, gdown_ref, sem.at[1])
-        last.start()
-        halves(lambda c: c.wait())
-        last.wait()
+            last = pltpu.make_async_copy(down_ref, gdown_ref, down_sem.at[0])
+            last.start()
+            halves(lambda c: c.wait(), lambda at: None)
+            last.wait()
 
 
 def mlp_bwd(lens, core, low, mid, cot, rest, wdown, vec, share, dp):
@@ -439,6 +454,7 @@
                 pltpu.VMEM((d, ff + 128), BF),
                 pltpu.SemaphoreType.DMA((2 * (ff // d) + 1,)),
                 pltpu.SemaphoreType.DMA((dp,)),
+                pltpu.SemaphoreType.DMA((max(1, d // (2 * share)),)),
             ],
         ),
         out_shape=[
@@ -456,7 +472,9 @@
 
 
 def attn_bwd_kernel(lens, core, x_ref, q_ref, k_ref, v_ref, gmix_ref, gmid_ref, lse_ref, inner_ref,
-                    w_ref, vec_ref, *rest, m, begin):
+                    w_hbm, vec_ref, *rest, m, begin):
+    *rest, w_ref, w_sem = rest
+    w_copy = pltpu.make_async_copy(w_hbm.at[:, 0:w_ref.shape[1]], w_ref, w_sem)
     if begin:
         dx_ref, gw_ref, acc_ref, gvec_ref, dk_ref, dv_ref, gq_ref = rest
     else:
@@ -469,6 +487,7 @@
 
     @pl.when(g == 0)
     def _():
+        w_copy.start()
         if not begin:
             pltpu.make_async_copy(prev_ref, before_ref, sem).start()
         acc_ref[...] = jnp.zeros_like(acc_ref)
@@ -537,6 +556,10 @@
         if ii:
             variant(ii, HALF)
 
+    @pl.when(i == end)
+    def _():
+        w_copy.wait()
+
     def finish(size):
         @pl.when(live & (part == (size == HALF)))
         def _():
@@ -620,7 +643,7 @@
                 pl.BlockSpec((1, ROWS, d), blk),
                 pl.BlockSpec((1, 16, ROWS), stat),
                 pl.BlockSpec((1, 16, ROWS), stat),
-                pl.BlockSpec(whole, fixed, pipeline_mode=one),
+                pl.BlockSpec(memory_space=pl.ANY),
                 pl.BlockSpec((8, d), fixed),
             ] + ([] if begin else [pl.BlockSpec(memory_space=pl.ANY)]),
             out_specs=[
@@ -633,7 +656,8 @@
                 pltpu.VMEM((rows, d), F32),
                 pltpu.VMEM((rows, d), F32),
                 pltpu.VMEM((ROWS, 3 * d), BF),
-            ] + ([] if begin else [pltpu.VMEM(wide, BF), pltpu.SemaphoreType.DMA(())]),
+            ] + ([] if begin else [pltpu.VMEM(wide, BF), pltpu.SemaphoreType.DMA(())])
+            + [pltpu.VMEM(whole, BF), pltpu.SemaphoreType.DMA(())],
         ),
         out_shape=[jax.ShapeDtypeStruct((1, rows, d), BF)]
         + ([jax.ShapeDtypeStruct(wide, BF)] if begin else [jax.ShapeDtypeStruct(split, BF)] * 2),

time: 735 us -> 733 us (level)
  no operation moved by 1% of the time
where the time goes in v2:
time: 733 us; the launch traced here: 728 us
  waiting for transfers between devices  241 us (33%)
  Pallas kernels  206 us (28%)
  starting transfers between devices  199 us (27%)
  local copies, waits for them, and re-layouts  43.9 us (6%)
  other arithmetic  23.6 us (3%)
  between operations  14.6 us (2%)
    ppermute x43, waiting for transfers between devices, swap(): return lax.ppermute(x, axis, [(s, s ^ bits) for s in range(size)])  241 us
    ppermute x43, starting transfers between devices, swap(): return lax.ppermute(x, axis, [(s, s ^ bits) for s in range(size)])  199 us
    pallas_call x1, Pallas kernels, mlp_bwd(): pl.pallas_call(functools.partial(mlp_bwd_kernel, share=share), grid_spec=...  59.3 us
    pallas_call x2, Pallas kernels, attn_bwd(): pl.pallas_call(functools.partial(attn_bwd_kernel, m=m, begin=begin), grid...  51.8 us
    pallas_call x1, Pallas kernels, attn_fwd(): pl.pallas_call(attn_fwd_kernel, grid_spec=pltpu.PrefetchScalarGridSpec(nu...  29.6 us
    pallas_call x2, Pallas kernels, place_weights(): pl.pallas_call(kernel, grid_spec=pltpu.PrefetchScalarGridSpec(num_scalar_...  26.3 us
    pallas_call x1, Pallas kernels, mlp_fwd(): pl.pallas_call(mlp_fwd_kernel, grid_spec=pltpu.PrefetchScalarGridSpec(num...  24.8 us
    gather x8, local copies, waits for them, and re-layouts, deal(): jnp.take(array, send_at[b * mb:(b + 1) * mb], axis=0, mode='clip')  19.5 us
  transfers between devices with their start and end apart: 44, of which 16 were waited for; matrix products, arithmetic and copies ran while one was open for 8% of the time, Pallas kernels for 14%

profile of v2, /device:TPU:0, one launch (start us, length us, event | category | flops | bytes accessed | tf_op | source)
XLA Modules:
  0.0 728.2 jit_solution(4451500043008343462)
XLA Ops:
  9.8 4.1 collective-permute-start.7
  23.3 2.6 collective-permute-done.6
  27.9 5.3 collective-permute-start.9
  37.7 3.4 gather_fusion.2
  41.1 3.4 gather_fusion.3
  45.9 3.4 gather_fusion.4
  50.9 3.4 gather_fusion.1
  55.1 11.7 %collective-permute-done.15 = bf16[24,6912]{1,0:T(8,128)(2,1)S(1)} collective-permute-done((bf16[24,6912]{1,0:T(8,128)(2,1)S(1)}, bf16[24,6912]{1,0:T(8,128)(2,1)S(1)}, u32[]{:S(2)}, u32[]{:S(2)}) %collective-permute-start.15) | collective-permute-done | bytes 331808 | tf_op jit(solution)/shard_map/ppermute | solution.py:777
  70.3 2.7 collective-permute-start.1
  74.6 10.8 %collective-permute-done.3.refs_1_ = bf16[2,256,768]{2,1,0:T(8,128)(2,1)S(1)} collective-permute-done((bf16[2,256,768]{2,1,0:T(8,128)(2,1)}, bf16[2,256,768]{2,1,0:T(8,128)(2,1)S(1)}, u32[]{:S(2)}, u32[]{:S(2)}) %collective-permute-start.3) | collective-permute-done | bytes 786464 | tf_op jit(solution)/shard_map/ppermute | solution.py:777
  85.4 5.4 collective-permute-start.2
  90.8 31.2 %collective-permute-done.4.refs_2_ = bf16[2,256,768]{2,1,0:T(8,128)(2,1)S(1)} collective-permute-done((bf16[2,256,768]{2,1,0:T(8,128)(2,1)}, bf16[2,256,768]{2,1,0:T(8,128)(2,1)S(1)}, u32[]{:S(2)}, u32[]{:S(2)}) %collective-permute-start.4) | collective-permute-done | bytes 786464 | tf_op jit(solution)/shard_map/ppermute | solution.py:777
  125.5 4.6 collective-permute-done.refs_1_
  130.1 2.9 collective-permute-start.18
  133.0 2.8 pad_maximum_fusion.1
  135.9 52.8 %collective-permute-done.1.refs_2_ = bf16[2,256,768]{2,1,0:T(8,128)(2,1)S(1)} collective-permute-done((bf16[2,256,768]{2,1,0:T(8,128)(2,1)}, bf16[2,256,768]{2,1,0:T(8,128)(2,1)S(1)}, u32[]{:S(2)}, u32[]{:S(2)}) %collective-permute-start.1) | collective-permute-done | bytes 786464 | tf_op jit(solution)/shard_map/ppermute | solution.py:777
  190.1 3.4 place_blocks.5
  193.6 3.5 place_blocks.4
  197.1 5.3 pad_maximum_fusion
  202.6 4.8 place_weights.2.w_ref.w_hbm
  209.1 29.6 %attn_fwd.1 = (bf16[2,1024,2304]{2,1,0:T(8,128)(2,1)}, bf16[2,1024,768]{2,1,0:T(8,128)(2,1)}, f32[2,16,1024]{2,1,0:T(8,128)}) custom-call(s32[2]{0:T(128)} %fusion.22.lens, bf16[2,1024,768]{2,1,0:T(8,128)(2,1)} %bitcast.137, bf16[768,2432]{1,0:T(8,128)(2,1)} %place_weights.2.w_ref.w_hbm, f32[8,768]{1,0:T(8,128)} %pad_convert_fusion.vec_ref), custom_call_target="tpu_custom_call" | custom-call | flops 60000002048 | bytes 20971520 | tf_op jit(solution)/shard_map/attn_fwd/pallas_call | solution.py:127
  238.7 21.5 %place_weights.3 = (bf16[768,3840]{1,0:T(8,128)(2,1)}, bf16[3072,768]{1,0:T(8,128)(2,1)}) custom-call(s32[32]{0:T(128)} %pad_add_fusion.at, bf16[16,24,6912]{2,1,0:T(8,128)(2,1)} %bitcast.28.refs_0_, bf16[16,24,6912]{2,1,0:T(8,128)(2,1)} %collective-permute-done.19.refs_1_), custom_call_target="tpu_custom_call" | custom-call | flops 8000000000 | bytes 21233664 | tf_op jit(solution)/shard_map/place_weights/pallas_call | solution.py:756
  260.2 24.8 %mlp_fwd.1 = (bf16[2,1024,768]{2,1,0:T(8,128)(2,1)}, f32[2,1024,768]{2,1,0:T(8,128)}) custom-call(s32[2]{0:T(128)} %fusion.22.lens, bf16[2,1024,768]{2,1,0:T(8,128)(2,1)} %get-tuple-element.30.low_ref, bf16[2,1024,768]{2,1,0:T(8,128)(2,1)} %bitcast.138, f32[8,768]{1,0:T(8,128)} %pad_convert_fusion.vec_ref, bf16[768,3840]{1,0:T(8,128)(2,1)} %get-tuple-element.31.rest_ref, ...), custom_call_target="tpu_custom_call" | custom-call | flops 40000000000 | bytes 41943040 | tf_op jit(solution)/shard_map/mlp_fwd/pallas_call | solution.py:246
  285.0 59.3 %mlp_bwd.1 = (f32[2,1024,768]{2,1,0:T(8,128)}, bf16[2,1024,768]{2,1,0:T(8,128)(2,1)}, f32[2,16,1024]{2,1,0:T(8,128)}, bf16[4,96,3840]{2,1,0:T(8,128)(2,1)}, bf16...) custom-call(s32[2]{0:T(128)} %fusion.22.lens, s32[1]{0:T(128)} %bitcast.35.core, ...), custom_call_target="tpu_custom_call" | custom-call | flops 80000000000 | bytes 62914560 | tf_op jit(solution)/shard_map/mlp_bwd/pallas_call | solution.py:423
  344.8 38.0 %attn_bwd.2 = (bf16[1,1024,768]{2,1,0:T(8,128)(2,1)}, bf16[768,2432]{1,0:T(8,128)(2,1)}) custom-call(s32[2]{0:T(128)} %fusion.22.lens, s32[1]{0:T(128)} %bitcast.35.core, bf16[2,1024,768]{2,1,0:T(8,128)(2,1)} %bitcast.139, bf16[2,1024,2304]{2,1,0:T(8,128)(2,1)} %get-tuple-element.35.q_ref.k_ref.v_ref, ...), custom_call_target="tpu_custom_call" | custom-call | flops 40000000000 | bytes 20971520 | tf_op jit(solution)/shard_map/attn_bwd/pallas_call | solution.py:632
  382.8 13.8 %attn_bwd.3 = (bf16[1,1024,768]{2,1,0:T(8,128)(2,1)}, bf16[4,96,2432]{2,1,0:T(8,128)(2,1)}, bf16[4,96,2432]{2,1,0:T(8,128)(2,1)}) custom-call(s32[2]{0:T(128)} %fusion.22.lens, s32[1]{0:T(128)} %bitcast.35.core, bf16[2,1024,768]{2,1,0:T(8,128)(2,1)} %bitcast.140, bf16[2,1024,2304]{2,1,0:T(8,128)(2,1)} %get-tuple-element.35.q_ref.k_ref.v_ref, ...), custom_call_target="tpu_custom_call" | custom-call | flops 40000000000 | bytes 20971520 | tf_op jit(solution)/shard_map/attn_bwd/pallas_call | solution.py:632
  396.5 2.3 dynamic-slice_bitcast_fusion.4
  398.9 75.7 %collective-permute-start.26 = (bf16[1,256,768]{2,1,0:T(8,128)(2,1)S(1)}, bf16[1,256,768]{2,1,0:T(8,128)(2,1)S(1)}, u32[]{:S(2)}, u32[]{:S(2)}) collective-permute-start(bf16[1,256,768]{2,1,0:T(8,128)(2,1)S(1)} %get-tuple-element.66), channel_id=1, source_target_pairs={{0,1},{1,0},{2,3},{3,2},{4,5},{5,4},{6,7},{7,6},{8,9},{9,8},{10,11... | collective-permute-start | bytes 1179656 | tf_op jit(solution)/shard_map/ppermute | solution.py:777
  474.6 7.0 collective-permute-start.27
  485.6 21.3 %collective-permute-done.27.refs_6_ = bf16[1,256,768]{2,1,0:T(8,128)(2,1)S(1)} collective-permute-done((bf16[1,256,768]{2,1,0:T(8,128)(2,1)S(1)}, bf16[1,256,768]{2,1,0:T(8,128)(2,1)S(1)}, u32[]{:S(2)}, u32[]{:S(2)}) %collective-permute-start.27) | collective-permute-done | bytes 393248 | tf_op jit(solution)/shard_map/ppermute | solution.py:777
  506.9 2.9 collective-permute-done.28.refs_7_
  509.8 2.6 collective-permute-start.25
  516.0 22.6 %collective-permute-start.20 = (bf16[2,256,768]{2,1,0:T(8,128)(2,1)}, bf16[2,256,768]{2,1,0:T(8,128)(2,1)S(1)}, u32[]{:S(2)}, u32[]{:S(2)}) collective-permute-start(bf16[2,256,768]{2,1,0:T(8,128)(2,1)} %get-tuple-element.62), channel_id=1, source_target_pairs={{0,1},{1,0},{2,3},{3,2},{4,5},{5,4},{6,7},{7,6},{8,9},{9,8},{10,11... | collective-permute-start | bytes 2359304 | tf_op jit(solution)/shard_map/ppermute | solution.py:777
  538.5 3.6 collective-permute-done.24.refs_2_
  544.2 3.4 place_blocks.7
  547.6 16.2 %collective-permute-done.20.refs_1_ = bf16[2,256,768]{2,1,0:T(8,128)(2,1)S(1)} collective-permute-done((bf16[2,256,768]{2,1,0:T(8,128)(2,1)}, bf16[2,256,768]{2,1,0:T(8,128)(2,1)S(1)}, u32[]{:S(2)}, u32[]{:S(2)}) %collective-permute-start.20) | collective-permute-done | bytes 786464 | tf_op jit(solution)/shard_map/ppermute | solution.py:777
  563.8 50.4 %collective-permute-done.21.refs_2_ = bf16[2,256,768]{2,1,0:T(8,128)(2,1)S(1)} collective-permute-done((bf16[2,256,768]{2,1,0:T(8,128)(2,1)}, bf16[2,256,768]{2,1,0:T(8,128)(2,1)S(1)}, u32[]{:S(2)}, u32[]{:S(2)}) %collective-permute-start.21) | collective-permute-done | bytes 786464 | tf_op jit(solution)/shard_map/ppermute | solution.py:777
  615.4 3.4 place_blocks.6
  618.9 2.5 fusion.11
  621.4 10.0 %collective-permute-start.30 = (bf16[96,2432]{1,0:T(8,128)(2,1)S(1)}, bf16[96,2432]{1,0:T(8,128)(2,1)S(1)}, u32[]{:S(2)}, u32[]{:S(2)}) collective-permute-start(bf16[96,2432]{1,0:T(8,128)(2,1)S(1)} %get-tuple-element.57), channel_id=1, source_target_pairs={{0,8},{4,12},{8,0},{12,4},{16,24},{20,28},{24,16},{28,20},{1,9},{5... | collective-permute-start | bytes 1400840 | tf_op jit(solution)/shard_map/ppermute | solution.py:777
  637.0 5.9 collective-permute-done.30
  642.9 16.0 %collective-permute-done.31 = bf16[96,2432]{1,0:T(8,128)(2,1)S(1)} collective-permute-done((bf16[96,2432]{1,0:T(8,128)(2,1)S(1)}, bf16[96,2432]{1,0:T(8,128)(2,1)S(1)}, u32[]{:S(2)}, u32[]{:S(2)}) %collective-permute-start.31) | collective-permute-done | bytes 466976 | tf_op jit(solution)/shard_map/ppermute | solution.py:777
  660.5 14.4 %collective-permute-start.33 = (bf16[24,2432]{1,0:T(8,128)(2,1)S(1)}, bf16[24,2432]{1,0:T(8,128)(2,1)S(1)}, u32[]{:S(2)}, u32[]{:S(2)}) collective-permute-start(bf16[24,2432]{1,0:T(8,128)(2,1)S(1)} %get-tuple-element.77), channel_id=1, source_target_pairs={{0,1},{1,0},{2,3},{3,2},{4,5},{5,4},{6,7},{7,6},{8,9},{9,8},{10,11... | collective-permute-start | bytes 350216 | tf_op jit(solution)/shard_map/ppermute | solution.py:777
  674.9 6.1 collective-permute-start.34
  684.0 16.1 %collective-permute-start.40 = (bf16[24,3840]{1,0:T(8,128)(2,1)S(1)}, bf16[24,3840]{1,0:T(8,128)(2,1)S(1)}, u32[]{:S(2)}, u32[]{:S(2)}) collective-permute-start(bf16[24,3840]{1,0:T(8,128)(2,1)S(1)} %get-tuple-element.74), channel_id=1, source_target_pairs={{0,1},{1,0},{2,3},{3,2},{4,5},{5,4},{6,7},{7,6},{8,9},{9,8},{10,11... | collective-permute-start | bytes 552968 | tf_op jit(solution)/shard_map/ppermute | solution.py:777
  700.2 2.4 collective-permute-start.42
  704.1 3.4 collective-permute-done.40
  707.5 6.1 collective-permute-done.41
  (161 shorter events, 64.8 us)
Async XLA Ops:
  7.2 707.9 %reduce-scatter.4.cloned.1.call-start = ((), (), s32[]{:S(2)}) async-start(), calls=%async_computation.1 | async-start | bytes 5068800
  9.8 13.5 %collective-permute-start.7 = (bf16[24,2432]{1,0:T(8,128)(2,1)}, bf16[24,2432]{1,0:T(8,128)(2,1)}, u32[]{:S(2)}, u32[]{:S(2)}) collective-permute-start(bf16[24,2432]{1,0:T(8,128)(2,1)} %get-tuple-element.83), channel_id=1, source_target_pairs={{0,2},{1,3},{2,0},{3,1},{4,6},{5,7},{6,4},{7,5},{8,10},{9,11},{10,... | collective-permute-start | bytes 350216 | tf_op jit(solution)/shard_map/ppermute | solution.py:777
  13.9 9.4 %collective-permute-start.8 = (bf16[24,2432]{1,0:T(8,128)(2,1)}, bf16[24,2432]{1,0:T(8,128)(2,1)}, u32[]{:S(2)}, u32[]{:S(2)}) collective-permute-start(bf16[24,2432]{1,0:T(8,128)(2,1)} %get-tuple-element.83), channel_id=1, source_target_pairs={{0,3},{1,2},{2,1},{3,0},{4,7},{5,6},{6,5},{7,4},{8,11},{9,10},{10,... | collective-permute-start | bytes 350216 | tf_op jit(solution)/shard_map/ppermute | solution.py:777
  15.2 10.6 %collective-permute-start.6 = (bf16[24,2432]{1,0:T(8,128)(2,1)}, bf16[24,2432]{1,0:T(8,128)(2,1)}, u32[]{:S(2)}, u32[]{:S(2)}) collective-permute-start(bf16[24,2432]{1,0:T(8,128)(2,1)} %get-tuple-element.83), channel_id=1, source_target_pairs={{0,1},{1,0},{2,3},{3,2},{4,5},{5,4},{6,7},{7,6},{8,9},{9,8},{10,11... | collective-permute-start | bytes 350216 | tf_op jit(solution)/shard_map/ppermute | solution.py:777
  18.1 36.1 %collective-permute-start.13 = (bf16[24,6912]{1,0:T(8,128)(2,1)S(1)}, bf16[24,6912]{1,0:T(8,128)(2,1)}, u32[]{:S(2)}, u32[]{:S(2)}) collective-permute-start(bf16[24,6912]{1,0:T(8,128)(2,1)S(1)} %constant_dynamic-update-slice_fusion), channel_id=1, source_target_pairs={{0,1},{1,0},{2,3},{3,2},{4,5},{5,4},{6,7},{7,6},{8,9},{9,8},{10,11... | collective-permute-start | bytes 995336 | tf_op jit(solution)/shard_map/ppermute | solution.py:777
  20.0 35.0 %collective-permute-start.14 = (bf16[24,6912]{1,0:T(8,128)(2,1)S(1)}, bf16[24,6912]{1,0:T(8,128)(2,1)}, u32[]{:S(2)}, u32[]{:S(2)}) collective-permute-start(bf16[24,6912]{1,0:T(8,128)(2,1)S(1)} %constant_dynamic-update-slice_fusion), channel_id=1, source_target_pairs={{0,2},{1,3},{2,0},{3,1},{4,6},{5,7},{6,4},{7,5},{8,10},{9,11},{10,... | collective-permute-start | bytes 995336 | tf_op jit(solution)/shard_map/ppermute | solution.py:777
  27.9 40.6 %collective-permute-start.9 = (bf16[4,24,2432]{2,1,0:T(8,128)(2,1)}, bf16[4,24,2432]{2,1,0:T(8,128)(2,1)}, u32[]{:S(2)}, u32[]{:S(2)}) collective-permute-start(bf16[4,24,2432]{2,1,0:T(8,128)(2,1)} %get-tuple-element.81), channel_id=1, source_target_pairs={{0,8},{4,12},{8,0},{12,4},{16,24},{20,28},{24,16},{28,20},{1,9},{5... | collective-permute-start | bytes 1400840 | tf_op jit(solution)/shard_map/ppermute | solution.py:777
  33.2 35.8 %collective-permute-start.10 = (bf16[4,24,2432]{2,1,0:T(8,128)(2,1)}, bf16[4,24,2432]{2,1,0:T(8,128)(2,1)}, u32[]{:S(2)}, u32[]{:S(2)}) collective-permute-start(bf16[4,24,2432]{2,1,0:T(8,128)(2,1)} %get-tuple-element.81), channel_id=1, source_target_pairs={{0,16},{4,20},{8,24},{12,28},{16,0},{20,4},{24,8},{28,12},{1,17},{... | collective-permute-start | bytes 1400840 | tf_op jit(solution)/shard_map/ppermute | solution.py:777
  34.7 35.5 %collective-permute-start.11 = (bf16[4,24,2432]{2,1,0:T(8,128)(2,1)}, bf16[4,24,2432]{2,1,0:T(8,128)(2,1)}, u32[]{:S(2)}, u32[]{:S(2)}) collective-permute-start(bf16[4,24,2432]{2,1,0:T(8,128)(2,1)} %get-tuple-element.81), channel_id=1, source_target_pairs={{0,24},{4,28},{8,16},{12,20},{16,8},{20,12},{24,0},{28,4},{1,25},{... | collective-permute-start | bytes 1400840 | tf_op jit(solution)/shard_map/ppermute | solution.py:777
  54.2 12.5 %collective-permute-start.15 = (bf16[24,6912]{1,0:T(8,128)(2,1)S(1)}, bf16[24,6912]{1,0:T(8,128)(2,1)S(1)}, u32[]{:S(2)}, u32[]{:S(2)}) collective-permute-start(bf16[24,6912]{1,0:T(8,128)(2,1)S(1)} %constant_dynamic-update-slice_fusion), channel_id=1, source_target_pairs={{0,3},{1,2},{2,1},{3,0},{4,7},{5,6},{6,5},{7,4},{8,11},{9,10},{10,... | collective-permute-start | bytes 995336 | tf_op jit(solution)/shard_map/ppermute | solution.py:777
  55.0 30.4 %collective-permute-start.3 = (bf16[2,256,768]{2,1,0:T(8,128)(2,1)}, bf16[2,256,768]{2,1,0:T(8,128)(2,1)S(1)}, u32[]{:S(2)}, u32[]{:S(2)}) collective-permute-start(bf16[2,256,768]{2,1,0:T(8,128)(2,1)} %gather_fusion.6), channel_id=1, source_target_pairs={{0,1},{1,0},{2,3},{3,2},{4,5},{5,4},{6,7},{7,6},{8,9},{9,8},{10,11... | collective-permute-start | bytes 2359304 | tf_op jit(solution)/shard_map/ppermute | solution.py:777
  66.8 55.2 %collective-permute-start.4 = (bf16[2,256,768]{2,1,0:T(8,128)(2,1)}, bf16[2,256,768]{2,1,0:T(8,128)(2,1)S(1)}, u32[]{:S(2)}, u32[]{:S(2)}) collective-permute-start(bf16[2,256,768]{2,1,0:T(8,128)(2,1)} %gather_fusion.7), channel_id=1, source_target_pairs={{0,2},{1,3},{2,0},{3,1},{4,6},{5,7},{6,4},{7,5},{8,10},{9,11},{10,... | collective-permute-start | bytes 2359304 | tf_op jit(solution)/shard_map/ppermute | solution.py:777
  68.6 55.4 %collective-permute-start.5 = (bf16[2,256,768]{2,1,0:T(8,128)(2,1)}, bf16[2,256,768]{2,1,0:T(8,128)(2,1)S(1)}, u32[]{:S(2)}, u32[]{:S(2)}) collective-permute-start(bf16[2,256,768]{2,1,0:T(8,128)(2,1)} %gather_fusion.8), channel_id=1, source_target_pairs={{0,3},{1,2},{2,1},{3,0},{4,7},{5,6},{6,5},{7,4},{8,11},{9,10},{10,... | collective-permute-start | bytes 2359304 | tf_op jit(solution)/shard_map/ppermute | solution.py:777
  69.0 61.1 %collective-permute-start = (bf16[2,256,768]{2,1,0:T(8,128)(2,1)}, bf16[2,256,768]{2,1,0:T(8,128)(2,1)S(1)}, u32[]{:S(2)}, u32[]{:S(2)}) collective-permute-start(bf16[2,256,768]{2,1,0:T(8,128)(2,1)} %gather_fusion.2), channel_id=1, source_target_pairs={{0,1},{1,0},{2,3},{3,2},{4,5},{5,4},{6,7},{7,6},{8,9},{9,8},{10,11... | collective-permute-start | bytes 2359304 | tf_op jit(solution)/shard_map/ppermute | solution.py:777
  70.3 118.4 %collective-permute-start.1 = (bf16[2,256,768]{2,1,0:T(8,128)(2,1)}, bf16[2,256,768]{2,1,0:T(8,128)(2,1)S(1)}, u32[]{:S(2)}, u32[]{:S(2)}) collective-permute-start(bf16[2,256,768]{2,1,0:T(8,128)(2,1)} %gather_fusion.3), channel_id=1, source_target_pairs={{0,2},{1,3},{2,0},{3,1},{4,6},{5,7},{6,4},{7,5},{8,10},{9,11},{10,... | collective-permute-start | bytes 2359304 | tf_op jit(solution)/shard_map/ppermute | solution.py:777
  73.0 60.1 %copy-start.4 = (bf16[1,4,24,2432]{3,2,1,0:T(8,128)(2,1)S(1)}, bf16[1,4,24,2432]{3,2,1,0:T(8,128)(2,1)}, u32[]{:S(2)}) copy-start(bf16[1,4,24,2432]{3,2,1,0:T(8,128)(2,1)} %get-tuple-element.80) | copy-start | bytes 1400836
  85.4 108.2 %collective-permute-start.2 = (bf16[2,256,768]{2,1,0:T(8,128)(2,1)S(1)}, bf16[2,256,768]{2,1,0:T(8,128)(2,1)}, u32[]{:S(2)}, u32[]{:S(2)}) collective-permute-start(bf16[2,256,768]{2,1,0:T(8,128)(2,1)S(1)} %copy-done.7), channel_id=1, source_target_pairs={{0,3},{1,2},{2,1},{3,0},{4,7},{5,6},{6,5},{7,4},{8,11},{9,10},{10,... | collective-permute-start | bytes 2359304 | tf_op jit(solution)/shard_map/ppermute | solution.py:777
  122.0 75.1 %collective-permute-start.16 = (bf16[4,24,6912]{2,1,0:T(8,128)(2,1)S(1)}, bf16[4,24,6912]{2,1,0:T(8,128)(2,1)}, u32[]{:S(2)}, u32[]{:S(2)}) collective-permute-start(bf16[4,24,6912]{2,1,0:T(8,128)(2,1)S(1)} %get-tuple-element.73), channel_id=1, source_target_pairs={{0,8},{4,12},{8,0},{12,4},{16,24},{20,28},{24,16},{28,20},{1,9},{5... | collective-permute-start | bytes 3981320 | tf_op jit(solution)/shard_map/ppermute | solution.py:777
  124.0 65.4 %copy-start.18 = (bf16[2,256,768]{2,1,0:T(8,128)(2,1)}, bf16[2,256,768]{2,1,0:T(8,128)(2,1)S(1)}, u32[]{:S(2)}) copy-start(bf16[2,256,768]{2,1,0:T(8,128)(2,1)S(1)} %collective-permute-done.5.refs_3_) | copy-start | bytes 2359300
  124.0 73.1 %collective-permute-start.17 = (bf16[4,24,6912]{2,1,0:T(8,128)(2,1)S(1)}, bf16[4,24,6912]{2,1,0:T(8,128)(2,1)}, u32[]{:S(2)}, u32[]{:S(2)}) collective-permute-start(bf16[4,24,6912]{2,1,0:T(8,128)(2,1)S(1)} %get-tuple-element.73), channel_id=1, source_target_pairs={{0,16},{4,20},{8,24},{12,28},{16,0},{20,4},{24,8},{28,12},{1,17},{... | collective-permute-start | bytes 3981320 | tf_op jit(solution)/shard_map/ppermute | solution.py:777
  130.1 67.0 %collective-permute-start.18 = (bf16[4,24,6912]{2,1,0:T(8,128)(2,1)S(1)}, bf16[4,24,6912]{2,1,0:T(8,128)(2,1)}, u32[]{:S(2)}, u32[]{:S(2)}) collective-permute-start(bf16[4,24,6912]{2,1,0:T(8,128)(2,1)S(1)} %get-tuple-element.73), channel_id=1, source_target_pairs={{0,24},{4,28},{8,16},{12,20},{16,8},{20,12},{24,0},{28,4},{1,25},{... | collective-permute-start | bytes 3981320 | tf_op jit(solution)/shard_map/ppermute | solution.py:777
  133.0 56.5 %copy-start.23 = (s32[1,8]{1,0:T(1,128)S(1)}, s32[1,8]{1,0:T(1,128)}, u32[]{:S(2)}) copy-start(s32[1,8]{1,0:T(1,128)} %param.14) | copy-start | bytes 100
  188.6 14.0 %collective-permute-start.12 = (bf16[16,24,2432]{2,1,0:T(8,128)(2,1)}, bf16[16,24,2432]{2,1,0:T(8,128)(2,1)}, u32[]{:S(2)}, u32[]{:S(2)}) collective-permute-start(bf16[16,24,2432]{2,1,0:T(8,128)(2,1)} %bitcast.16.refs_0_), channel_id=1, source_target_pairs={{0,4},{4,0},{8,12},{12,8},{16,20},{20,16},{24,28},{28,24},{1,5},{5... | collective-permute-start | bytes 5603336 | tf_op jit(solution)/shard_map/ppermute | solution.py:777
  202.4 36.3 %collective-permute-start.19 = (bf16[16,24,6912]{2,1,0:T(8,128)(2,1)}, bf16[16,24,6912]{2,1,0:T(8,128)(2,1)}, u32[]{:S(2)}, u32[]{:S(2)}) collective-permute-start(bf16[16,24,6912]{2,1,0:T(8,128)(2,1)} %bitcast.28.refs_0_), channel_id=1, source_target_pairs={{0,4},{4,0},{8,12},{12,8},{16,20},{20,16},{24,28},{28,24},{1,5},{5... | collective-permute-start | bytes 15925256 | tf_op jit(solution)/shard_map/ppermute | solution.py:777
  344.4 288.5 %collective-permute-start.36 = (bf16[4,96,3840]{2,1,0:T(8,128)(2,1)}, bf16[4,96,3840]{2,1,0:T(8,128)(2,1)}, u32[]{:S(2)}, u32[]{:S(2)}) collective-permute-start(bf16[4,96,3840]{2,1,0:T(8,128)(2,1)} %get-tuple-element.48), channel_id=1, source_target_pairs={{0,4},{4,0},{8,12},{12,8},{16,20},{20,16},{24,28},{28,24},{1,5},{5... | collective-permute-start | bytes 8847368 | tf_op jit(solution)/shard_map/ppermute | solution.py:777
  396.5 86.5 %copy-start.5 = (bf16[1,1024,768]{2,1,0:T(8,128)(2,1)S(1)}, bf16[1,1024,768]{2,1,0:T(8,128)(2,1)}, u32[]{:S(2)}) copy-start(bf16[1,1024,768]{2,1,0:T(8,128)(2,1)} %get-tuple-element.42) | copy-start | bytes 4718596
  398.9 86.7 %collective-permute-start.26 = (bf16[1,256,768]{2,1,0:T(8,128)(2,1)S(1)}, bf16[1,256,768]{2,1,0:T(8,128)(2,1)S(1)}, u32[]{:S(2)}, u32[]{:S(2)}) collective-permute-start(bf16[1,256,768]{2,1,0:T(8,128)(2,1)S(1)} %get-tuple-element.66), channel_id=1, source_target_pairs={{0,1},{1,0},{2,3},{3,2},{4,5},{5,4},{6,7},{7,6},{8,9},{9,8},{10,11... | collective-permute-start | bytes 1179656 | tf_op jit(solution)/shard_map/ppermute | solution.py:777
  474.6 32.3 %collective-permute-start.27 = (bf16[1,256,768]{2,1,0:T(8,128)(2,1)S(1)}, bf16[1,256,768]{2,1,0:T(8,128)(2,1)S(1)}, u32[]{:S(2)}, u32[]{:S(2)}) collective-permute-start(bf16[1,256,768]{2,1,0:T(8,128)(2,1)S(1)} %get-tuple-element.65), channel_id=1, source_target_pairs={{0,2},{1,3},{2,0},{3,1},{4,6},{5,7},{6,4},{7,5},{8,10},{9,11},{10,... | collective-permute-start | bytes 1179656 | tf_op jit(solution)/shard_map/ppermute | solution.py:777
  481.5 28.3 %collective-permute-start.28 = (bf16[1,256,768]{2,1,0:T(8,128)(2,1)S(1)}, bf16[1,256,768]{2,1,0:T(8,128)(2,1)S(1)}, u32[]{:S(2)}, u32[]{:S(2)}) collective-permute-start(bf16[1,256,768]{2,1,0:T(8,128)(2,1)S(1)} %get-tuple-element.64), channel_id=1, source_target_pairs={{0,3},{1,2},{2,1},{3,0},{4,7},{5,6},{6,5},{7,4},{8,11},{9,10},{10,... | collective-permute-start | bytes 1179656 | tf_op jit(solution)/shard_map/ppermute | solution.py:777
  483.0 135.9 %collective-permute-start.29 = (bf16[4,96,2432]{2,1,0:T(8,128)(2,1)}, bf16[4,96,2432]{2,1,0:T(8,128)(2,1)}, u32[]{:S(2)}, u32[]{:S(2)}) collective-permute-start(bf16[4,96,2432]{2,1,0:T(8,128)(2,1)} %get-tuple-element.46), channel_id=1, source_target_pairs={{0,4},{4,0},{8,12},{12,8},{16,20},{20,16},{24,28},{28,24},{1,5},{5... | collective-permute-start | bytes 5603336 | tf_op jit(solution)/shard_map/ppermute | solution.py:777
  485.6 30.4 %collective-permute-start.23 = (bf16[1,256,768]{2,1,0:T(8,128)(2,1)}, bf16[1,256,768]{2,1,0:T(8,128)(2,1)}, u32[]{:S(2)}, u32[]{:S(2)}) collective-permute-start(bf16[1,256,768]{2,1,0:T(8,128)(2,1)} %get-tuple-element.70), channel_id=1, source_target_pairs={{0,1},{1,0},{2,3},{3,2},{4,5},{5,4},{6,7},{7,6},{8,9},{9,8},{10,11... | collective-permute-start | bytes 1179656 | tf_op jit(solution)/shard_map/ppermute | solution.py:777
  506.9 35.3 %collective-permute-start.24 = (bf16[1,256,768]{2,1,0:T(8,128)(2,1)}, bf16[1,256,768]{2,1,0:T(8,128)(2,1)}, u32[]{:S(2)}, u32[]{:S(2)}) collective-permute-start(bf16[1,256,768]{2,1,0:T(8,128)(2,1)} %get-tuple-element.69), channel_id=1, source_target_pairs={{0,2},{1,3},{2,0},{3,1},{4,6},{5,7},{6,4},{7,5},{8,10},{9,11},{10,... | collective-permute-start | bytes 1179656 | tf_op jit(solution)/shard_map/ppermute | solution.py:777
  509.8 32.4 %collective-permute-start.25 = (bf16[1,256,768]{2,1,0:T(8,128)(2,1)S(1)}, bf16[1,256,768]{2,1,0:T(8,128)(2,1)}, u32[]{:S(2)}, u32[]{:S(2)}) collective-permute-start(bf16[1,256,768]{2,1,0:T(8,128)(2,1)S(1)} %get-tuple-element.68), channel_id=1, source_target_pairs={{0,3},{1,2},{2,1},{3,0},{4,7},{5,6},{6,5},{7,4},{8,11},{9,10},{10,... | collective-permute-start | bytes 1179656 | tf_op jit(solution)/shard_map/ppermute | solution.py:777
  516.0 47.9 %collective-permute-start.20 = (bf16[2,256,768]{2,1,0:T(8,128)(2,1)}, bf16[2,256,768]{2,1,0:T(8,128)(2,1)S(1)}, u32[]{:S(2)}, u32[]{:S(2)}) collective-permute-start(bf16[2,256,768]{2,1,0:T(8,128)(2,1)} %get-tuple-element.62), channel_id=1, source_target_pairs={{0,1},{1,0},{2,3},{3,2},{4,5},{5,4},{6,7},{7,6},{8,9},{9,8},{10,11... | collective-permute-start | bytes 2359304 | tf_op jit(solution)/shard_map/ppermute | solution.py:777
  542.2 72.1 %collective-permute-start.21 = (bf16[2,256,768]{2,1,0:T(8,128)(2,1)}, bf16[2,256,768]{2,1,0:T(8,128)(2,1)S(1)}, u32[]{:S(2)}, u32[]{:S(2)}) collective-permute-start(bf16[2,256,768]{2,1,0:T(8,128)(2,1)} %get-tuple-element.61), channel_id=1, source_target_pairs={{0,2},{1,3},{2,0},{3,1},{4,6},{5,7},{6,4},{7,5},{8,10},{9,11},{10,... | collective-permute-start | bytes 2359304 | tf_op jit(solution)/shard_map/ppermute | solution.py:777
  542.2 72.1 %collective-permute-start.22 = (bf16[2,256,768]{2,1,0:T(8,128)(2,1)}, bf16[2,256,768]{2,1,0:T(8,128)(2,1)S(1)}, u32[]{:S(2)}, u32[]{:S(2)}) collective-permute-start(bf16[2,256,768]{2,1,0:T(8,128)(2,1)} %get-tuple-element.60), channel_id=1, source_target_pairs={{0,3},{1,2},{2,1},{3,0},{4,7},{5,6},{6,5},{7,4},{8,11},{9,10},{10,... | collective-permute-start | bytes 2359304 | tf_op jit(solution)/shard_map/ppermute | solution.py:777
  621.4 21.5 %collective-permute-start.30 = (bf16[96,2432]{1,0:T(8,128)(2,1)S(1)}, bf16[96,2432]{1,0:T(8,128)(2,1)S(1)}, u32[]{:S(2)}, u32[]{:S(2)}) collective-permute-start(bf16[96,2432]{1,0:T(8,128)(2,1)S(1)} %get-tuple-element.57), channel_id=1, source_target_pairs={{0,8},{4,12},{8,0},{12,4},{16,24},{20,28},{24,16},{28,20},{1,9},{5... | collective-permute-start | bytes 1400840 | tf_op jit(solution)/shard_map/ppermute | solution.py:777
  631.4 27.6 %collective-permute-start.31 = (bf16[96,2432]{1,0:T(8,128)(2,1)S(1)}, bf16[96,2432]{1,0:T(8,128)(2,1)S(1)}, u32[]{:S(2)}, u32[]{:S(2)}) collective-permute-start(bf16[96,2432]{1,0:T(8,128)(2,1)S(1)} %get-tuple-element.59), channel_id=1, source_target_pairs={{0,16},{4,20},{8,24},{12,28},{16,0},{20,4},{24,8},{28,12},{1,17},{... | collective-permute-start | bytes 1400840 | tf_op jit(solution)/shard_map/ppermute | solution.py:777
  631.4 27.6 %collective-permute-start.32 = (bf16[96,2432]{1,0:T(8,128)(2,1)S(1)}, bf16[96,2432]{1,0:T(8,128)(2,1)S(1)}, u32[]{:S(2)}, u32[]{:S(2)}) collective-permute-start(bf16[96,2432]{1,0:T(8,128)(2,1)S(1)} %get-tuple-element.58), channel_id=1, source_target_pairs={{0,24},{4,28},{8,16},{12,20},{16,8},{20,12},{24,0},{28,4},{1,25},{... | collective-permute-start | bytes 1400840 | tf_op jit(solution)/shard_map/ppermute | solution.py:777
  635.0 46.0 %collective-permute-start.37 = (bf16[96,3840]{1,0:T(8,128)(2,1)S(1)}, bf16[96,3840]{1,0:T(8,128)(2,1)S(1)}, u32[]{:S(2)}, u32[]{:S(2)}) collective-permute-start(bf16[96,3840]{1,0:T(8,128)(2,1)S(1)} %get-tuple-element.54), channel_id=1, source_target_pairs={{0,8},{4,12},{8,0},{12,4},{16,24},{20,28},{24,16},{28,20},{1,9},{5... | collective-permute-start | bytes 2211848 | tf_op jit(solution)/shard_map/ppermute | solution.py:777
  637.0 45.4 %collective-permute-start.38 = (bf16[96,3840]{1,0:T(8,128)(2,1)S(1)}, bf16[96,3840]{1,0:T(8,128)(2,1)S(1)}, u32[]{:S(2)}, u32[]{:S(2)}) collective-permute-start(bf16[96,3840]{1,0:T(8,128)(2,1)S(1)} %get-tuple-element.56), channel_id=1, source_target_pairs={{0,16},{4,20},{8,24},{12,28},{16,0},{20,4},{24,8},{28,12},{1,17},{... | collective-permute-start | bytes 2211848 | tf_op jit(solution)/shard_map/ppermute | solution.py:777
  642.9 39.5 %collective-permute-start.39 = (bf16[96,3840]{1,0:T(8,128)(2,1)S(1)}, bf16[96,3840]{1,0:T(8,128)(2,1)S(1)}, u32[]{:S(2)}, u32[]{:S(2)}) collective-permute-start(bf16[96,3840]{1,0:T(8,128)(2,1)S(1)} %get-tuple-element.55), channel_id=1, source_target_pairs={{0,24},{4,28},{8,16},{12,20},{16,8},{20,12},{24,0},{28,4},{1,25},{... | collective-permute-start | bytes 2211848 | tf_op jit(solution)/shard_map/ppermute | solution.py:777
  660.5 39.7 %collective-permute-start.33 = (bf16[24,2432]{1,0:T(8,128)(2,1)S(1)}, bf16[24,2432]{1,0:T(8,128)(2,1)S(1)}, u32[]{:S(2)}, u32[]{:S(2)}) collective-permute-start(bf16[24,2432]{1,0:T(8,128)(2,1)S(1)} %get-tuple-element.77), channel_id=1, source_target_pairs={{0,1},{1,0},{2,3},{3,2},{4,5},{5,4},{6,7},{7,6},{8,9},{9,8},{10,11... | collective-permute-start | bytes 350216 | tf_op jit(solution)/shard_map/ppermute | solution.py:777
  674.9 27.7 %collective-permute-start.34 = (bf16[24,2432]{1,0:T(8,128)(2,1)S(1)}, bf16[24,2432]{1,0:T(8,128)(2,1)S(1)}, u32[]{:S(2)}, u32[]{:S(2)}) collective-permute-start(bf16[24,2432]{1,0:T(8,128)(2,1)S(1)} %get-tuple-element.79), channel_id=1, source_target_pairs={{0,2},{1,3},{2,0},{3,1},{4,6},{5,7},{6,4},{7,5},{8,10},{9,11},{10,... | collective-permute-start | bytes 350216 | tf_op jit(solution)/shard_map/ppermute | solution.py:777
  681.0 21.6 %collective-permute-start.35 = (bf16[24,2432]{1,0:T(8,128)(2,1)S(1)}, bf16[24,2432]{1,0:T(8,128)(2,1)S(1)}, u32[]{:S(2)}, u32[]{:S(2)}) collective-permute-start(bf16[24,2432]{1,0:T(8,128)(2,1)S(1)} %get-tuple-element.78), channel_id=1, source_target_pairs={{0,3},{1,2},{2,1},{3,0},{4,7},{5,6},{6,5},{7,4},{8,11},{9,10},{10,... | collective-permute-start | bytes 350216 | tf_op jit(solution)/shard_map/ppermute | solution.py:777
  684.0 23.5 %collective-permute-start.40 = (bf16[24,3840]{1,0:T(8,128)(2,1)S(1)}, bf16[24,3840]{1,0:T(8,128)(2,1)S(1)}, u32[]{:S(2)}, u32[]{:S(2)}) collective-permute-start(bf16[24,3840]{1,0:T(8,128)(2,1)S(1)} %get-tuple-element.74), channel_id=1, source_target_pairs={{0,1},{1,0},{2,3},{3,2},{4,5},{5,4},{6,7},{7,6},{8,9},{9,8},{10,11... | collective-permute-start | bytes 552968 | tf_op jit(solution)/shard_map/ppermute | solution.py:777
  700.2 13.5 %collective-permute-start.41 = (bf16[24,3840]{1,0:T(8,128)(2,1)S(1)}, bf16[24,3840]{1,0:T(8,128)(2,1)S(1)}, u32[]{:S(2)}, u32[]{:S(2)}) collective-permute-start(bf16[24,3840]{1,0:T(8,128)(2,1)S(1)} %get-tuple-element.76), channel_id=1, source_target_pairs={{0,2},{1,3},{2,0},{3,1},{4,6},{5,7},{6,4},{7,5},{8,10},{9,11},{10,... | collective-permute-start | bytes 552968 | tf_op jit(solution)/shard_map/ppermute | solution.py:777
  700.2 13.4 %collective-permute-start.42 = (bf16[24,3840]{1,0:T(8,128)(2,1)S(1)}, bf16[24,3840]{1,0:T(8,128)(2,1)S(1)}, u32[]{:S(2)}, u32[]{:S(2)}) collective-permute-start(bf16[24,3840]{1,0:T(8,128)(2,1)S(1)} %get-tuple-element.75), channel_id=1, source_target_pairs={{0,3},{1,2},{2,1},{3,0},{4,7},{5,6},{6,5},{7,4},{8,11},{9,10},{10,... | collective-permute-start | bytes 552968 | tf_op jit(solution)/shard_map/ppermute | solution.py:777
  (20 other events, 314.7 us)
Sparse Core Ops, SparseCore 0:
  512.5 149.3 reduce-scatter.3
